TPU v7x, 32 devices: a whole 2x2x4 slice. The times are simulated.
32 devices in a mesh: layer: 4 (over y, core), feat: 8 (over z, x).
Axes of the slice: x: 2, y: 2, z: 4, core: 2. Of those that a mesh axis runs over, the one named last changes fastest.
Arguments:
- acts: bfloat16 [4, 384, 2048], P('layer', 'feat'), may hold values from -64 to 64
- errors: bfloat16 [4, 384, 2048], P('layer', 'feat'), may hold values from -2.390625 to 2.390625
- enc_weight: bfloat16 [4, 2048, 8192], P('layer', None, 'feat'), may hold values from -0.0625 to 0.0625
- dec_weight: bfloat16 [4, 8192, 2048], P('layer', 'feat'), may hold values from -0.125 to 0.125
- chosen: int32 [384, 32], replicated, may hold values from 0 to 8191, all different within a row
Outputs:
- dec_grad: bfloat16 [4, 8192, 2048], P('layer', 'feat')
- enc_grad: bfloat16 [4, 2048, 8192], P('layer', None, 'feat')
Inputs may be any that keep to these rules, and one draw needn't show every extreme that they name: `chosen`: each row names 32 different features.
All inputs are finite; a program needn't handle non-finite values.
Results may differ from a plain program's by a relative error of at most 0.02.
Values may be sent and summed in bfloat16 or wider, within the bound.
No kernel may reach another device: no remote copies, remote signals or barrier semaphores. Data moves between devices by JAX's collectives and lax.ppermute only.
A program may use at most 64 MiB of HBM per device.

v0:
```python
import functools

import jax
import jax.numpy as jnp
from jax import lax
from jax.experimental import pallas as pl
from jax.experimental.pallas import tpu as pltpu
from jax.sharding import PartitionSpec as P


LANES = 128
VECTOR_FLOPS = 1024
SUB = 8
F32 = jnp.float32
BF16 = jnp.bfloat16


def pack_kernel(starts, chosen, tgt, held):
    k, tokens = chosen.shape
    quarter = tgt.shape[0]
    n_chunks = starts.shape[0] - 1
    rows = tokens // n_chunks
    held[:, :k] = chosen[...].T - starts[0]
    for p in range(n_chunks):
        q, r0 = divmod(p * rows, quarter)
        tgt[r0 : r0 + rows, q * k : (q + 1) * k] = held[pl.ds(pl.multiple_of(starts[1 + p], SUB), rows), :k]


def index_kernel(k, groups, tgt, inv):
    width = inv.shape[1]
    quarter = tgt.shape[0]
    column = lax.broadcasted_iota(jnp.int32, (SUB, width), 1)

    def body(m, _):
        ids = tgt[pl.ds(pl.multiple_of(m * SUB, SUB), SUB), :]
        for n, q in enumerate(groups):
            out = jnp.full((SUB, width), -1, jnp.int32)
            for j in range(k):
                lane = q * k + j
                out = jnp.where(ids[:, lane : lane + 1] == column, lane, out)
            inv[pl.ds(pl.multiple_of(n * quarter + m * SUB, SUB), SUB), :] = out
        return 0

    lax.fori_loop(0, quarter // SUB, body, 0)


def pick(dense, ids, out, groups, first_block, k):
    width = dense.shape[1]
    per = LANES // k
    quarter = ids.shape[0]
    lane_group = lax.broadcasted_iota(jnp.int32, (SUB, LANES), 1) // k
    blocks = width // LANES
    picked = []
    for m in range(quarter // SUB):
        want = ids[m * SUB : (m + 1) * SUB, :]
        low = jnp.bitwise_and(want, LANES - 1)
        key = jnp.right_shift(want, 7) * per + lane_group
        value = out[m]
        for h in range(blocks):
            for q in groups:
                t = (q - groups[0]) * quarter + m * SUB
                got = jnp.take_along_axis(
                    dense[t : t + SUB, h * LANES : (h + 1) * LANES], low, axis=1
                )
                value = jnp.where(key == (first_block + h) * per + q, got, value)
        picked.append(value)
    return picked


def expand(vals, inv, first, size):
    tokens = inv.shape[0]
    quarter = vals[0].shape[0] * len(vals)
    rows_out = []
    for t in range(0, tokens, SUB):
        source = vals[t % quarter // SUB]
        parts = []
        for h in range(size // LANES):
            at = inv[t : t + SUB, first + h * LANES : first + (h + 1) * LANES]
            got = jnp.take_along_axis(source, jnp.bitwise_and(at, LANES - 1), axis=1)
            parts.append(jnp.where(at >= 0, got, 0.0))
        rows_out.append(jnp.concatenate(parts, axis=1))
    return jnp.concatenate(rows_out, axis=0)


def row_blocks(ref):
    return [ref[m : m + SUB, :] for m in range(0, ref.shape[0], SUB)]


def stacked(chunks):
    return jnp.concatenate([chunk[0] for chunk in chunks], axis=0)


def pre_kernel(n_chunks, groups, k, block, *refs):
    chunks = refs[:n_chunks]
    weight, ids, vals = refs[n_chunks:]
    rows = stacked(chunks)
    acc = [jnp.zeros((SUB, LANES), F32)] * (ids.shape[0] // SUB)
    for j in range(0, weight.shape[2], block):
        dense = jnp.dot(rows, weight[0, :, j : j + block], preferred_element_type=F32)
        acc = pick(dense, ids, acc, groups, j // LANES, k)
    vals[...] = jnp.concatenate(acc, axis=0).astype(vals.dtype)


def turn_kernel(n_chunks, *refs):
    chunks = refs[:n_chunks]
    squares, turned = refs[n_chunks:]
    rows = stacked(chunks)
    turned[...] = rows.T
    tokens, width = rows.shape
    values = rows.astype(F32)
    total = jnp.sum((values * values).reshape(tokens // SUB, SUB, width), axis=0)
    part = total[:, :LANES]
    for j in range(LANES, width, LANES):
        part = part + total[:, j : j + LANES]
    squares[...] = part


def scale_of(squares, count):
    return 2.0 / (jnp.sum(squares[...]) / count + 1e-6)


def code_grad_kernel(n_chunks, groups, k, block, first, last, count, *refs):
    refs = list(refs)
    chunks = [refs.pop(0) for _ in range(n_chunks)]
    weight, ids = refs.pop(0), refs.pop(0)
    before = None if first else refs.pop(0)
    squares = refs.pop(0) if last else None
    (vals,) = refs
    rows = stacked(chunks)
    quarter = ids.shape[0]
    acc = [jnp.zeros((SUB, LANES), F32)] * (quarter // SUB) if first else row_blocks(before)
    for j in range(0, weight.shape[1], block):
        dense = lax.dot_general(
            rows, weight[0, j : j + block, :], (((1,), (1,)), ((), ())), preferred_element_type=F32
        )
        acc = pick(dense, ids, acc, groups, j // LANES, k)
    out = jnp.concatenate(acc, axis=0)
    if last:
        out = out * scale_of(squares, count)
    vals[...] = out.astype(vals.dtype)


def total_of(parts):
    total = parts[0][...].astype(F32)
    for part in parts[1:]:
        total = total + part[...].astype(F32)
    return total


def split_rows(value):
    return [value[m : m + SUB] for m in range(0, value.shape[0], SUB)]


def dec_grad_kernel(n_chunks, n_parts, block, count, *refs):
    chunks = refs[:n_chunks]
    parts = refs[n_chunks : n_chunks + n_parts]
    *inv, squares, out, held, sems = refs[n_chunks + n_parts :]
    vals = split_rows(total_of(parts) * scale_of(squares, count))
    rows = stacked(chunks)
    copies = []
    for n, j in enumerate(range(0, inv[0].shape[1], block)):
        codes = jnp.concatenate([expand(vals, half, j, block) for half in inv], axis=0).T.astype(BF16)
        held[j : j + block, :] = jnp.dot(codes, rows, preferred_element_type=F32).astype(BF16)
        copies.append(
            pltpu.make_async_copy(held.at[pl.ds(j, block), :], out.at[0, pl.ds(j, block), :], sems.at[n])
        )
        copies[-1].start()
    for copy in copies:
        copy.wait()


def enc_grad_kernel(n_parts, block, tall, *refs):
    parts = refs[:n_parts]
    turned, *inv, out, held, sems = refs[n_parts:]
    vals = split_rows(total_of(parts))
    copies = []
    for n, j in enumerate(range(0, inv[0].shape[1], block)):
        pre_grad = jnp.concatenate([expand(vals, half, j, block) for half in inv], axis=0).astype(BF16)
        for m in range(0, turned.shape[0], tall):
            held[m : m + tall, j : j + block] = jnp.dot(
                turned[m : m + tall, :], pre_grad, preferred_element_type=F32
            ).astype(BF16)
        copies.append(
            pltpu.make_async_copy(held.at[:, pl.ds(j, block)], out.at[0, :, pl.ds(j, block)], sems.at[n])
        )
        copies[-1].start()
    for copy in copies:
        copy.wait()


VMEM = pl.BlockSpec(memory_space=pltpu.VMEM)
SMEM = pl.BlockSpec(memory_space=pltpu.SMEM)
ANY = pl.BlockSpec(memory_space=pl.ANY)


def call(kernel, args, in_specs, out_specs, out_shape, scratch, flops, nbytes):
    return pl.pallas_call(
        kernel,
        in_specs=in_specs,
        out_specs=out_specs,
        out_shape=out_shape,
        scratch_shapes=scratch,
        compiler_params=pltpu.CompilerParams(vmem_limit_bytes=24 << 20),
        cost_estimate=pl.CostEstimate(
            flops=flops, bytes_accessed=nbytes, transcendentals=0
        ),
    )(*args)


def on_device_ops(outer, inner, n_layer, acts, errors, enc_weight, dec_weight, chosen):
    feat = outer * inner
    rows, width = acts.shape[1], acts.shape[2]
    feat_dev = enc_weight.shape[2]
    tokens, k = chosen.shape
    quarter = tokens // (LANES // k)
    me = lax.axis_index("feat")
    my_outer, my_inner = me // inner, me % inner
    places = [(o, i) for o in range(outer) for i in range(inner)]

    def ring(by):
        return [(o * inner + i, (o + by) % outer * inner + i) for o, i in places]

    def turn(by):
        return [(o * inner + i, o * inner + (i + by) % inner) for o, i in places]

    def send(x, pairs):
        return lax.ppermute(x, "feat", pairs)

    right, left = steps_of(outer)

    def gather(x, last_by_ring):
        fronts, sides = [x], [[send(x, turn(c)) for c in range(1, inner)]]
        for n in range(1, right + 1):
            fronts.append(send(fronts[-1], ring(1)))
            if n == right and last_by_ring:
                sides.append([send(y, ring(1)) for y in sides[-1]])
            else:
                sides.append([send(fronts[-1], turn(c)) for c in range(1, inner)])
        held = x
        for _ in range(1, left + 1):
            held = send(held, ring(-1))
            fronts.append(held)
            sides.append([send(held, turn(c)) for c in range(1, inner)])
        return [y for front, side in zip(fronts, sides) for y in (front, *side)]

    starts = [me * feat_dev]
    for by in [*range(right + 1), *(-n for n in range(1, left + 1))]:
        for c in range(inner):
            o = (my_outer - by + outer) % outer
            i = (my_inner - c + inner) % inner
            starts.append((o * inner + i) * rows)
    starts = jnp.stack(starts).astype(jnp.int32)

    a = gather(acts, False)
    e = gather(errors, True)

    shape = jax.ShapeDtypeStruct
    per = LANES // k
    block = min(256, feat_dev)
    tgt = call(
        pack_kernel, (starts, chosen.T), [SMEM, VMEM], VMEM,
        shape((quarter, LANES), jnp.int32), [pltpu.VMEM((tokens, LANES), jnp.int32)],
        tokens * k, 4 * tokens * LANES,
    )
    halves = [tuple(range(per // 2)), tuple(range(per // 2, per))]
    per_half = feat // 2
    half_tokens = tokens // 2
    half_flops = 2 * half_tokens * width * feat_dev
    half_bytes = 2 * width * half_tokens
    inv = []
    for groups in halves:
        inv.append(
            call(
                functools.partial(index_kernel, k, groups), (tgt,), [VMEM], VMEM,
                shape((half_tokens, feat_dev), jnp.int32), [],
                VECTOR_FLOPS * half_tokens * k * feat_dev, 4 * half_tokens * feat_dev,
            )
        )

    def exchange(value):
        parts = [value]
        for s in range(1, n_layer):
            pairs = [(d, (d + s) % n_layer) for d in range(n_layer)]
            parts.append(lax.ppermute(value, "layer", pairs))
        return parts

    args = (*a, enc_weight, tgt)
    vals = call(
        functools.partial(pre_kernel, feat, tuple(range(per)), k, block),
        args, [VMEM] * len(args), VMEM, shape((quarter, LANES), BF16),
        [], 2 * half_flops, 2 * half_bytes,
    )
    squares, turned = call(
        functools.partial(turn_kernel, feat), a, [VMEM] * feat, [VMEM, VMEM],
        [shape((SUB, LANES), F32), shape((width, tokens), BF16)],
        [], 2 * tokens * width, 4 * half_bytes,
    )
    pre_parts = exchange(vals)

    vals = []
    for n, groups in enumerate(halves):
        first, last = n == 0, n == len(halves) - 1
        args = (*e[n * per_half : (n + 1) * per_half], dec_weight, tgt, *vals, *([squares] if last else []))
        vals = [
            call(
                functools.partial(
                    code_grad_kernel, per_half, groups, k, block, first, last, tokens * width
                ),
                args, [VMEM] * len(args), VMEM, shape((quarter, LANES), BF16 if last else F32),
                [], half_flops, half_bytes,
            )
        ]
    grad_parts = exchange(vals[0])

    def out_scratch(rows, columns):
        return [pltpu.VMEM((rows, columns), BF16), pltpu.SemaphoreType.DMA((feat_dev // block,))]

    args = (*e, *pre_parts, *inv, squares)
    dec_grad = call(
        functools.partial(dec_grad_kernel, feat, n_layer, block, tokens * width),
        args, [VMEM] * len(args), ANY, shape((1, feat_dev, width), BF16),
        out_scratch(feat_dev, width), 2 * half_flops, 2 * feat_dev * width,
    )
    args = (*grad_parts, turned, *inv)
    enc_grad = call(
        functools.partial(enc_grad_kernel, n_layer, block, min(512, width)),
        args, [VMEM] * len(args), ANY, shape((1, width, feat_dev), BF16),
        out_scratch(width, feat_dev), 2 * half_flops, 2 * feat_dev * width,
    )
    return (dec_grad, enc_grad)


def steps_of(outer):
    return outer // 2, outer - 1 - outer // 2


def solution(mesh):
    feat, n_layer = mesh.shape["feat"], mesh.shape["layer"]
    inner = 2 if feat % 2 == 0 else 1

    return jax.shard_map(
        functools.partial(on_device_ops, feat // inner, inner, n_layer),
        mesh=mesh,
        in_specs=(
            P("layer", "feat", None),
            P("layer", "feat", None),
            P("layer", None, "feat"),
            P("layer", "feat", None),
            P(),
        ),
        out_specs=(P("layer", "feat", None), P("layer", None, "feat")),
        check_vma=False,
    )
```

profile of v0, /device:TPU:0, one launch (start us, length us, event | category | flops | bytes accessed | tf_op | source)
XLA Modules:
  0.0 58.1 jit_solution(13287186945807223589)
XLA Ops:
  0.6 3.1 %collective-permute-start.8 = (bf16[1,48,2048]{2,1,0:T(8,128)(2,1)}, bf16[1,48,2048]{2,1,0:T(8,128)(2,1)S(1)}, u32[]{:S(2)}, u32[]{:S(2)}) collective-permute-start(bf16[1,48,2048]{2,1,0:T(8,128)(2,1)} %refs_0_.5), channel_id=1, source_target_pairs={{0,2},{1,3},{2,4},{3,5},{4,6},{5,7},{6,0},{7,1},{8,10},{9,11},{10,... | collective-permute-start | bytes 589832 | tf_op jit(solution)/shard_map/ppermute | solution.py:227
  3.7 2.1 %collective-permute-start.12 = (bf16[1,48,2048]{2,1,0:T(8,128)(2,1)}, bf16[1,48,2048]{2,1,0:T(8,128)(2,1)S(1)}, u32[]{:S(2)}, u32[]{:S(2)}) collective-permute-start(bf16[1,48,2048]{2,1,0:T(8,128)(2,1)} %refs_0_.5), channel_id=1, source_target_pairs={{0,6},{1,7},{2,0},{3,1},{4,2},{5,3},{6,4},{7,5},{8,14},{9,15},{10,... | collective-permute-start | bytes 589832 | tf_op jit(solution)/shard_map/ppermute | solution.py:227
  5.8 1.6 %collective-permute-start.7 = (bf16[1,48,2048]{2,1,0:T(8,128)(2,1)}, bf16[1,48,2048]{2,1,0:T(8,128)(2,1)S(1)}, u32[]{:S(2)}, u32[]{:S(2)}) collective-permute-start(bf16[1,48,2048]{2,1,0:T(8,128)(2,1)} %refs_0_.5), channel_id=1, source_target_pairs={{0,1},{1,0},{2,3},{3,2},{4,5},{5,4},{6,7},{7,6},{8,9},{9,8},{10,11... | collective-permute-start | bytes 589832 | tf_op jit(solution)/shard_map/ppermute | solution.py:227
  7.5 1.8 %collective-permute-start.5 = (bf16[1,48,2048]{2,1,0:T(8,128)(2,1)}, bf16[1,48,2048]{2,1,0:T(8,128)(2,1)S(1)}, u32[]{:S(2)}, u32[]{:S(2)}) collective-permute-start(bf16[1,48,2048]{2,1,0:T(8,128)(2,1)} %refs_0_.7), channel_id=1, source_target_pairs={{0,6},{1,7},{2,0},{3,1},{4,2},{5,3},{6,4},{7,5},{8,14},{9,15},{10,... | collective-permute-start | bytes 589832 | tf_op jit(solution)/shard_map/ppermute | solution.py:227
  9.3 0.2 collective-permute-start.1
  9.6 0.8 %copy-done.3 = s32[384,32]{0,1:T(8,128)S(1)} copy-done((s32[384,32]{0,1:T(8,128)S(1)}, s32[384,32]{0,1:T(8,128)}, u32[]{:S(2)}) %copy-start.3) | copy-done | bytes 49176
  10.4 0.8 %shard_map.68.refs_9_.tgt.refs_5_ = s32[96,128]{1,0:T(8,128)S(1)} custom-call(s32[9]{0:T(128)S(1)} %stack.39.starts, s32[32,384]{1,0:T(8,128)S(1)} %bitcast.10), custom_call_target="tpu_custom_call" | custom-call | flops 12288 | bytes 196608 | tf_op jit(solution)/shard_map/pallas_call | solution.py:197
  11.2 0.6 collective-permute-done.8.refs_2_
  11.8 6.8 %collective-permute-start.10 = (bf16[1,48,2048]{2,1,0:T(8,128)(2,1)S(1)}, bf16[1,48,2048]{2,1,0:T(8,128)(2,1)S(1)}, u32[]{:S(2)}, u32[]{:S(2)}) collective-permute-start(bf16[1,48,2048]{2,1,0:T(8,128)(2,1)S(1)} %collective-permute-done.8.refs_2_), channel_id=1, source_target_pairs={{0,2},{1,3},{2,4},{3,5},{4,6},{5,7},{6,0},{7,1},{8,10},{9,11},{10,... | collective-permute-start | bytes 589832 | tf_op jit(solution)/shard_map/ppermute | solution.py:227
  18.6 2.5 %shard_map.71.refs_13_.refs_6_ = s32[192,1024]{1,0:T(8,128)S(1)} custom-call(s32[96,128]{1,0:T(8,128)S(1)} %shard_map.68.refs_9_.tgt.refs_5_), custom_call_target="tpu_custom_call" | custom-call | flops 6442450944 | bytes 786432 | tf_op jit(solution)/shard_map/pallas_call | solution.py:197
  21.1 1.9 %collective-permute-start = (bf16[1,48,2048]{2,1,0:T(8,128)(2,1)S(1)}, bf16[1,48,2048]{2,1,0:T(8,128)(2,1)S(1)}, u32[]{:S(2)}, u32[]{:S(2)}) collective-permute-start(bf16[1,48,2048]{2,1,0:T(8,128)(2,1)S(1)} %copy-done.1), channel_id=1, source_target_pairs={{0,1},{1,0},{2,3},{3,2},{4,5},{5,4},{6,7},{7,6},{8,9},{9,8},{10,11... | collective-permute-start | bytes 589832 | tf_op jit(solution)/shard_map/ppermute | solution.py:227
  23.0 0.2 collective-permute-start.9
  23.2 1.8 %collective-permute-start.13 = (bf16[1,48,2048]{2,1,0:T(8,128)(2,1)S(1)}, bf16[1,48,2048]{2,1,0:T(8,128)(2,1)S(1)}, u32[]{:S(2)}, u32[]{:S(2)}) collective-permute-start(bf16[1,48,2048]{2,1,0:T(8,128)(2,1)S(1)} %collective-permute-done.12.refs_6_), channel_id=1, source_target_pairs={{0,1},{1,0},{2,3},{3,2},{4,5},{5,4},{6,7},{7,6},{8,9},{9,8},{10,11... | collective-permute-start | bytes 589832 | tf_op jit(solution)/shard_map/ppermute | solution.py:227
  25.0 1.1 %collective-permute-start.2 = (bf16[1,48,2048]{2,1,0:T(8,128)(2,1)S(1)}, bf16[1,48,2048]{2,1,0:T(8,128)(2,1)S(1)}, u32[]{:S(2)}, u32[]{:S(2)}) collective-permute-start(bf16[1,48,2048]{2,1,0:T(8,128)(2,1)S(1)} %collective-permute-done.1.refs_2_), channel_id=1, source_target_pairs={{0,1},{1,0},{2,3},{3,2},{4,5},{5,4},{6,7},{7,6},{8,9},{9,8},{10,11... | collective-permute-start | bytes 589832 | tf_op jit(solution)/shard_map/ppermute | solution.py:227
  26.1 1.7 %collective-permute-done.10.refs_4_ = bf16[1,48,2048]{2,1,0:T(8,128)(2,1)S(1)} collective-permute-done((bf16[1,48,2048]{2,1,0:T(8,128)(2,1)S(1)}, bf16[1,48,2048]{2,1,0:T(8,128)(2,1)S(1)}, u32[]{:S(2)}, u32[]{:S(2)}) %collective-permute-start.10) | collective-permute-done | bytes 196640 | tf_op jit(solution)/shard_map/ppermute | solution.py:227
  27.8 1.5 %collective-permute-start.11 = (bf16[1,48,2048]{2,1,0:T(8,128)(2,1)S(1)}, bf16[1,48,2048]{2,1,0:T(8,128)(2,1)S(1)}, u32[]{:S(2)}, u32[]{:S(2)}) collective-permute-start(bf16[1,48,2048]{2,1,0:T(8,128)(2,1)S(1)} %collective-permute-done.10.refs_4_), channel_id=1, source_target_pairs={{0,1},{1,0},{2,3},{3,2},{4,5},{5,4},{6,7},{7,6},{8,9},{9,8},{10,11... | collective-permute-start | bytes 589832 | tf_op jit(solution)/shard_map/ppermute | solution.py:227
  29.3 2.5 %shard_map.70.refs_12_.refs_5_ = s32[192,1024]{1,0:T(8,128)S(1)} custom-call(s32[96,128]{1,0:T(8,128)S(1)} %shard_map.68.refs_9_.tgt.refs_5_), custom_call_target="tpu_custom_call" | custom-call | flops 6442450944 | bytes 786432 | tf_op jit(solution)/shard_map/pallas_call | solution.py:197
  31.8 0.7 %collective-permute-start.3 = (bf16[1,48,2048]{2,1,0:T(8,128)(2,1)S(1)}, bf16[1,48,2048]{2,1,0:T(8,128)(2,1)S(1)}, u32[]{:S(2)}, u32[]{:S(2)}) collective-permute-start(bf16[1,48,2048]{2,1,0:T(8,128)(2,1)S(1)} %collective-permute-done.1.refs_2_), channel_id=1, source_target_pairs={{0,2},{1,3},{2,4},{3,5},{4,6},{5,7},{6,0},{7,1},{8,10},{9,11},{10,... | collective-permute-start | bytes 589832 | tf_op jit(solution)/shard_map/ppermute | solution.py:227
  32.5 4.3 %collective-permute-done.13.refs_7_ = bf16[1,48,2048]{2,1,0:T(8,128)(2,1)S(1)} collective-permute-done((bf16[1,48,2048]{2,1,0:T(8,128)(2,1)S(1)}, bf16[1,48,2048]{2,1,0:T(8,128)(2,1)S(1)}, u32[]{:S(2)}, u32[]{:S(2)}) %collective-permute-start.13) | collective-permute-done | bytes 196640 | tf_op jit(solution)/shard_map/ppermute | solution.py:227
  36.7 2.3 %collective-permute-start.6 = (bf16[1,48,2048]{2,1,0:T(8,128)(2,1)S(1)}, bf16[1,48,2048]{2,1,0:T(8,128)(2,1)S(1)}, u32[]{:S(2)}, u32[]{:S(2)}) collective-permute-start(bf16[1,48,2048]{2,1,0:T(8,128)(2,1)S(1)} %collective-permute-done.5.refs_6_.refs_2_), channel_id=1, source_target_pairs={{0,1},{1,0},{2,3},{3,2},{4,5},{5,4},{6,7},{7,6},{8,9},{9,8},{10,11... | collective-permute-start | bytes 589832 | tf_op jit(solution)/shard_map/ppermute | solution.py:227
  39.1 0.4 collective-permute-done.2.refs_3_
  39.5 0.8 %collective-permute-start.4 = (bf16[1,48,2048]{2,1,0:T(8,128)(2,1)S(1)}, bf16[1,48,2048]{2,1,0:T(8,128)(2,1)S(1)}, u32[]{:S(2)}, u32[]{:S(2)}) collective-permute-start(bf16[1,48,2048]{2,1,0:T(8,128)(2,1)S(1)} %collective-permute-done.2.refs_3_), channel_id=1, source_target_pairs={{0,2},{1,3},{2,4},{3,5},{4,6},{5,7},{6,0},{7,1},{8,10},{9,11},{10,... | collective-permute-start | bytes 589832 | tf_op jit(solution)/shard_map/ppermute | solution.py:227
  40.3 1.7 %shard_map.74.refs_6_ = f32[96,128]{1,0:T(8,128)S(1)} custom-call(bf16[1,48,2048]{2,1,0:T(8,128)(2,1)S(1)} %copy-done.1, bf16[1,48,2048]{2,1,0:T(8,128)(2,1)S(1)} %collective-permute-done.refs_1_, bf16[1,48,2048]{2,1,0:T(8,128)(2,1)S(1)} %collective-permute-done.1.refs_2_, bf16[1,48,2048]{2,1,0:T(8,128)(2,1)S(1)} %collective-permute-done.2.refs_3_, ...), custom_call_target="tpu_custom_call" | custom-call | flops 805306368 | bytes 786432 | tf_op jit(solution)/shard_map/pallas_call | solution.py:197
  42.0 2.0 %shard_map.69.refs_8_ = bf16[96,128]{1,0:T(8,128)(2,1)S(1)} custom-call(bf16[1,48,2048]{2,1,0:T(8,128)(2,1)S(1)} %copy-done.2, bf16[1,48,2048]{2,1,0:T(8,128)(2,1)S(1)} %collective-permute-done.7.refs_1_, bf16[1,48,2048]{2,1,0:T(8,128)(2,1)S(1)} %collective-permute-done.8.refs_2_, bf16[1,48,2048]{2,1,0:T(8,128)(2,1)S(1)} %collective-permute-done.9.refs_3_, ...), custom_call_target="tpu_custom_call" | custom-call | flops 1610612736 | bytes 1572864 | tf_op jit(solution)/shard_map/pallas_call | solution.py:197
  44.1 1.6 %collective-permute-start.15 = (bf16[96,128]{1,0:T(8,128)(2,1)S(1)}, bf16[96,128]{1,0:T(8,128)(2,1)S(1)}, u32[]{:S(2)}, u32[]{:S(2)}) collective-permute-start(bf16[96,128]{1,0:T(8,128)(2,1)S(1)} %shard_map.69.refs_8_), channel_id=1, source_target_pairs={{0,16},{8,24},{16,0},{24,8},{1,17},{9,25},{17,1},{25,9},{2,18},{10... | collective-permute-start | bytes 73736 | tf_op jit(solution)/shard_map/ppermute | solution.py:284
  45.7 0.5 shard_map.72
  46.4 0.6 %collective-permute-done.4.refs_5_.refs_1_ = bf16[1,48,2048]{2,1,0:T(8,128)(2,1)S(1)} collective-permute-done((bf16[1,48,2048]{2,1,0:T(8,128)(2,1)S(1)}, bf16[1,48,2048]{2,1,0:T(8,128)(2,1)S(1)}, u32[]{:S(2)}, u32[]{:S(2)}) %collective-permute-start.4) | collective-permute-done | bytes 196640 | tf_op jit(solution)/shard_map/ppermute | solution.py:227
  47.0 1.7 %shard_map.75.refs_0_ = bf16[96,128]{1,0:T(8,128)(2,1)S(1)} custom-call(bf16[1,48,2048]{2,1,0:T(8,128)(2,1)S(1)} %collective-permute-done.3.refs_4_.refs_0_, bf16[1,48,2048]{2,1,0:T(8,128)(2,1)S(1)} %collective-permute-done.4.refs_5_.refs_1_, bf16[1,48,2048]{2,1,0:T(8,128)(2,1)S(1)} %collective-permute-done.5.refs_6_.refs_2_, ...), custom_call_target="tpu_custom_call" | custom-call | flops 805306368 | bytes 786432 | tf_op jit(solution)/shard_map/pallas_call | solution.py:197
  48.7 1.0 %collective-permute-start.19 = (bf16[96,128]{1,0:T(8,128)(2,1)S(1)}, bf16[96,128]{1,0:T(8,128)(2,1)S(1)}, u32[]{:S(2)}, u32[]{:S(2)}) collective-permute-start(bf16[96,128]{1,0:T(8,128)(2,1)S(1)} %shard_map.75.refs_0_), channel_id=1, source_target_pairs={{0,24},{8,0},{16,8},{24,16},{1,25},{9,1},{17,9},{25,17},{2,26},{10... | collective-permute-start | bytes 73736 | tf_op jit(solution)/shard_map/ppermute | solution.py:284
  49.8 0.6 %collective-permute-start.18 = (bf16[96,128]{1,0:T(8,128)(2,1)S(1)}, bf16[96,128]{1,0:T(8,128)(2,1)S(1)}, u32[]{:S(2)}, u32[]{:S(2)}) collective-permute-start(bf16[96,128]{1,0:T(8,128)(2,1)S(1)} %shard_map.75.refs_0_), channel_id=1, source_target_pairs={{0,16},{8,24},{16,0},{24,8},{1,17},{9,25},{17,1},{25,9},{2,18},{10... | collective-permute-start | bytes 73736 | tf_op jit(solution)/shard_map/ppermute | solution.py:284
  50.5 3.9 %shard_map.73 = bf16[1,1024,2048]{2,1,0:T(8,128)(2,1)} custom-call(bf16[1,48,2048]{2,1,0:T(8,128)(2,1)S(1)} %copy-done.1, bf16[1,48,2048]{2,1,0:T(8,128)(2,1)S(1)} %collective-permute-done.refs_1_, bf16[1,48,2048]{2,1,0:T(8,128)(2,1)S(1)} %collective-permute-done.1.refs_2_, bf16[1,48,2048]{2,1,0:T(8,128)(2,1)S(1)} %collective-permute-done.2.refs_3_, ...), custom_call_target="tpu_custom_call" | custom-call | flops 1610612736 | bytes 4194304 | tf_op jit(solution)/shard_map/pallas_call | solution.py:197
  54.5 3.6 %shard_map.76 = bf16[1,2048,1024]{2,1,0:T(8,128)(2,1)} custom-call(bf16[96,128]{1,0:T(8,128)(2,1)S(1)} %shard_map.75.refs_0_, bf16[96,128]{1,0:T(8,128)(2,1)S(1)} %collective-permute-done.17.refs_1_, bf16[96,128]{1,0:T(8,128)(2,1)S(1)} %collective-permute-done.18.refs_2_, bf16[96,128]{1,0:T(8,128)(2,1)S(1)} %collective-permute-done.19.refs_3_, ...), custom_call_target="tpu_custom_call" | custom-call | flops 1610612736 | bytes 4194304 | tf_op jit(solution)/shard_map/pallas_call | solution.py:197
  (28 shorter events, 0.6 us)
Async XLA Ops:
  0.6 11.1 %collective-permute-start.8 = (bf16[1,48,2048]{2,1,0:T(8,128)(2,1)}, bf16[1,48,2048]{2,1,0:T(8,128)(2,1)S(1)}, u32[]{:S(2)}, u32[]{:S(2)}) collective-permute-start(bf16[1,48,2048]{2,1,0:T(8,128)(2,1)} %refs_0_.5), channel_id=1, source_target_pairs={{0,2},{1,3},{2,4},{3,5},{4,6},{5,7},{6,0},{7,1},{8,10},{9,11},{10,... | collective-permute-start | bytes 589832 | tf_op jit(solution)/shard_map/ppermute | solution.py:227
  3.7 17.4 %collective-permute-start.12 = (bf16[1,48,2048]{2,1,0:T(8,128)(2,1)}, bf16[1,48,2048]{2,1,0:T(8,128)(2,1)S(1)}, u32[]{:S(2)}, u32[]{:S(2)}) collective-permute-start(bf16[1,48,2048]{2,1,0:T(8,128)(2,1)} %refs_0_.5), channel_id=1, source_target_pairs={{0,6},{1,7},{2,0},{3,1},{4,2},{5,3},{6,4},{7,5},{8,14},{9,15},{10,... | collective-permute-start | bytes 589832 | tf_op jit(solution)/shard_map/ppermute | solution.py:227
  5.8 17.2 %collective-permute-start.7 = (bf16[1,48,2048]{2,1,0:T(8,128)(2,1)}, bf16[1,48,2048]{2,1,0:T(8,128)(2,1)S(1)}, u32[]{:S(2)}, u32[]{:S(2)}) collective-permute-start(bf16[1,48,2048]{2,1,0:T(8,128)(2,1)} %refs_0_.5), channel_id=1, source_target_pairs={{0,1},{1,0},{2,3},{3,2},{4,5},{5,4},{6,7},{7,6},{8,9},{9,8},{10,11... | collective-permute-start | bytes 589832 | tf_op jit(solution)/shard_map/ppermute | solution.py:227
  7.5 15.8 %collective-permute-start.5 = (bf16[1,48,2048]{2,1,0:T(8,128)(2,1)}, bf16[1,48,2048]{2,1,0:T(8,128)(2,1)S(1)}, u32[]{:S(2)}, u32[]{:S(2)}) collective-permute-start(bf16[1,48,2048]{2,1,0:T(8,128)(2,1)} %refs_0_.7), channel_id=1, source_target_pairs={{0,6},{1,7},{2,0},{3,1},{4,2},{5,3},{6,4},{7,5},{8,14},{9,15},{10,... | collective-permute-start | bytes 589832 | tf_op jit(solution)/shard_map/ppermute | solution.py:227
  9.3 15.8 %collective-permute-start.1 = (bf16[1,48,2048]{2,1,0:T(8,128)(2,1)}, bf16[1,48,2048]{2,1,0:T(8,128)(2,1)S(1)}, u32[]{:S(2)}, u32[]{:S(2)}) collective-permute-start(bf16[1,48,2048]{2,1,0:T(8,128)(2,1)} %refs_0_.7), channel_id=1, source_target_pairs={{0,2},{1,3},{2,4},{3,5},{4,6},{5,7},{6,0},{7,1},{8,10},{9,11},{10,... | collective-permute-start | bytes 589832 | tf_op jit(solution)/shard_map/ppermute | solution.py:227
  9.6 0.8 %copy-start.3 = (s32[384,32]{0,1:T(8,128)S(1)}, s32[384,32]{0,1:T(8,128)}, u32[]{:S(2)}) copy-start(s32[384,32]{0,1:T(8,128)} %param.9) | copy-start | bytes 147460
  11.2 9.9 %copy-start.1 = (bf16[1,48,2048]{2,1,0:T(8,128)(2,1)S(1)}, bf16[1,48,2048]{2,1,0:T(8,128)(2,1)}, u32[]{:S(2)}) copy-start(bf16[1,48,2048]{2,1,0:T(8,128)(2,1)} %refs_0_.7) | copy-start | bytes 589828
  11.8 16.0 %collective-permute-start.10 = (bf16[1,48,2048]{2,1,0:T(8,128)(2,1)S(1)}, bf16[1,48,2048]{2,1,0:T(8,128)(2,1)S(1)}, u32[]{:S(2)}, u32[]{:S(2)}) collective-permute-start(bf16[1,48,2048]{2,1,0:T(8,128)(2,1)S(1)} %collective-permute-done.8.refs_2_), channel_id=1, source_target_pairs={{0,2},{1,3},{2,4},{3,5},{4,6},{5,7},{6,0},{7,1},{8,10},{9,11},{10,... | collective-permute-start | bytes 589832 | tf_op jit(solution)/shard_map/ppermute | solution.py:227
  21.1 19.2 %copy-start = (bf16[1,1024,2048]{2,1,0:T(8,128)(2,1)S(1)}, bf16[1,1024,2048]{2,1,0:T(8,128)(2,1)}, u32[]{:S(2)}) copy-start(bf16[1,1024,2048]{2,1,0:T(8,128)(2,1)} %refs_4_.3) | copy-start | bytes 12582916
  21.1 10.7 %collective-permute-start = (bf16[1,48,2048]{2,1,0:T(8,128)(2,1)S(1)}, bf16[1,48,2048]{2,1,0:T(8,128)(2,1)S(1)}, u32[]{:S(2)}, u32[]{:S(2)}) collective-permute-start(bf16[1,48,2048]{2,1,0:T(8,128)(2,1)S(1)} %copy-done.1), channel_id=1, source_target_pairs={{0,1},{1,0},{2,3},{3,2},{4,5},{5,4},{6,7},{7,6},{8,9},{9,8},{10,11... | collective-permute-start | bytes 589832 | tf_op jit(solution)/shard_map/ppermute | solution.py:227
  23.0 19.0 %collective-permute-start.9 = (bf16[1,48,2048]{2,1,0:T(8,128)(2,1)S(1)}, bf16[1,48,2048]{2,1,0:T(8,128)(2,1)S(1)}, u32[]{:S(2)}, u32[]{:S(2)}) collective-permute-start(bf16[1,48,2048]{2,1,0:T(8,128)(2,1)S(1)} %collective-permute-done.8.refs_2_), channel_id=1, source_target_pairs={{0,1},{1,0},{2,3},{3,2},{4,5},{5,4},{6,7},{7,6},{8,9},{9,8},{10,11... | collective-permute-start | bytes 589832 | tf_op jit(solution)/shard_map/ppermute | solution.py:227
  23.2 13.5 %collective-permute-start.13 = (bf16[1,48,2048]{2,1,0:T(8,128)(2,1)S(1)}, bf16[1,48,2048]{2,1,0:T(8,128)(2,1)S(1)}, u32[]{:S(2)}, u32[]{:S(2)}) collective-permute-start(bf16[1,48,2048]{2,1,0:T(8,128)(2,1)S(1)} %collective-permute-done.12.refs_6_), channel_id=1, source_target_pairs={{0,1},{1,0},{2,3},{3,2},{4,5},{5,4},{6,7},{7,6},{8,9},{9,8},{10,11... | collective-permute-start | bytes 589832 | tf_op jit(solution)/shard_map/ppermute | solution.py:227
  25.0 14.5 %collective-permute-start.2 = (bf16[1,48,2048]{2,1,0:T(8,128)(2,1)S(1)}, bf16[1,48,2048]{2,1,0:T(8,128)(2,1)S(1)}, u32[]{:S(2)}, u32[]{:S(2)}) collective-permute-start(bf16[1,48,2048]{2,1,0:T(8,128)(2,1)S(1)} %collective-permute-done.1.refs_2_), channel_id=1, source_target_pairs={{0,1},{1,0},{2,3},{3,2},{4,5},{5,4},{6,7},{7,6},{8,9},{9,8},{10,11... | collective-permute-start | bytes 589832 | tf_op jit(solution)/shard_map/ppermute | solution.py:227
  27.8 14.2 %collective-permute-start.11 = (bf16[1,48,2048]{2,1,0:T(8,128)(2,1)S(1)}, bf16[1,48,2048]{2,1,0:T(8,128)(2,1)S(1)}, u32[]{:S(2)}, u32[]{:S(2)}) collective-permute-start(bf16[1,48,2048]{2,1,0:T(8,128)(2,1)S(1)} %collective-permute-done.10.refs_4_), channel_id=1, source_target_pairs={{0,1},{1,0},{2,3},{3,2},{4,5},{5,4},{6,7},{7,6},{8,9},{9,8},{10,11... | collective-permute-start | bytes 589832 | tf_op jit(solution)/shard_map/ppermute | solution.py:227
  31.8 10.3 %copy-start.2 = (bf16[1,48,2048]{2,1,0:T(8,128)(2,1)S(1)}, bf16[1,48,2048]{2,1,0:T(8,128)(2,1)}, u32[]{:S(2)}) copy-start(bf16[1,48,2048]{2,1,0:T(8,128)(2,1)} %refs_0_.5) | copy-start | bytes 589828
  31.8 10.3 %copy-start.4 = (bf16[1,2048,1024]{2,1,0:T(8,128)(2,1)S(1)}, bf16[1,2048,1024]{2,1,0:T(8,128)(2,1)}, u32[]{:S(2)}) copy-start(bf16[1,2048,1024]{2,1,0:T(8,128)(2,1)} %refs_8_.1) | copy-start | bytes 12582916
  31.8 14.6 %collective-permute-start.3 = (bf16[1,48,2048]{2,1,0:T(8,128)(2,1)S(1)}, bf16[1,48,2048]{2,1,0:T(8,128)(2,1)S(1)}, u32[]{:S(2)}, u32[]{:S(2)}) collective-permute-start(bf16[1,48,2048]{2,1,0:T(8,128)(2,1)S(1)} %collective-permute-done.1.refs_2_), channel_id=1, source_target_pairs={{0,2},{1,3},{2,4},{3,5},{4,6},{5,7},{6,0},{7,1},{8,10},{9,11},{10,... | collective-permute-start | bytes 589832 | tf_op jit(solution)/shard_map/ppermute | solution.py:227
  36.7 9.4 %collective-permute-start.6 = (bf16[1,48,2048]{2,1,0:T(8,128)(2,1)S(1)}, bf16[1,48,2048]{2,1,0:T(8,128)(2,1)S(1)}, u32[]{:S(2)}, u32[]{:S(2)}) collective-permute-start(bf16[1,48,2048]{2,1,0:T(8,128)(2,1)S(1)} %collective-permute-done.5.refs_6_.refs_2_), channel_id=1, source_target_pairs={{0,1},{1,0},{2,3},{3,2},{4,5},{5,4},{6,7},{7,6},{8,9},{9,8},{10,11... | collective-permute-start | bytes 589832 | tf_op jit(solution)/shard_map/ppermute | solution.py:227
  39.5 7.5 %collective-permute-start.4 = (bf16[1,48,2048]{2,1,0:T(8,128)(2,1)S(1)}, bf16[1,48,2048]{2,1,0:T(8,128)(2,1)S(1)}, u32[]{:S(2)}, u32[]{:S(2)}) collective-permute-start(bf16[1,48,2048]{2,1,0:T(8,128)(2,1)S(1)} %collective-permute-done.2.refs_3_), channel_id=1, source_target_pairs={{0,2},{1,3},{2,4},{3,5},{4,6},{5,7},{6,0},{7,1},{8,10},{9,11},{10,... | collective-permute-start | bytes 589832 | tf_op jit(solution)/shard_map/ppermute | solution.py:227
  44.0 6.4 %collective-permute-start.16 = (bf16[96,128]{1,0:T(8,128)(2,1)S(1)}, bf16[96,128]{1,0:T(8,128)(2,1)S(1)}, u32[]{:S(2)}, u32[]{:S(2)}) collective-permute-start(bf16[96,128]{1,0:T(8,128)(2,1)S(1)} %shard_map.69.refs_8_), channel_id=1, source_target_pairs={{0,24},{8,0},{16,8},{24,16},{1,25},{9,1},{17,9},{25,17},{2,26},{10... | collective-permute-start | bytes 73736 | tf_op jit(solution)/shard_map/ppermute | solution.py:284
  44.1 6.4 %collective-permute-start.15 = (bf16[96,128]{1,0:T(8,128)(2,1)S(1)}, bf16[96,128]{1,0:T(8,128)(2,1)S(1)}, u32[]{:S(2)}, u32[]{:S(2)}) collective-permute-start(bf16[96,128]{1,0:T(8,128)(2,1)S(1)} %shard_map.69.refs_8_), channel_id=1, source_target_pairs={{0,16},{8,24},{16,0},{24,8},{1,17},{9,25},{17,1},{25,9},{2,18},{10... | collective-permute-start | bytes 73736 | tf_op jit(solution)/shard_map/ppermute | solution.py:284
  46.2 4.4 %collective-permute-start.14 = (bf16[96,128]{1,0:T(8,128)(2,1)S(1)}, bf16[96,128]{1,0:T(8,128)(2,1)S(1)}, u32[]{:S(2)}, u32[]{:S(2)}) collective-permute-start(bf16[96,128]{1,0:T(8,128)(2,1)S(1)} %shard_map.69.refs_8_), channel_id=1, source_target_pairs={{0,8},{8,16},{16,24},{24,0},{1,9},{9,17},{17,25},{25,1},{2,10},{10... | collective-permute-start | bytes 73736 | tf_op jit(solution)/shard_map/ppermute | solution.py:284
  48.7 5.7 %collective-permute-start.19 = (bf16[96,128]{1,0:T(8,128)(2,1)S(1)}, bf16[96,128]{1,0:T(8,128)(2,1)S(1)}, u32[]{:S(2)}, u32[]{:S(2)}) collective-permute-start(bf16[96,128]{1,0:T(8,128)(2,1)S(1)} %shard_map.75.refs_0_), channel_id=1, source_target_pairs={{0,24},{8,0},{16,8},{24,16},{1,25},{9,1},{17,9},{25,17},{2,26},{10... | collective-permute-start | bytes 73736 | tf_op jit(solution)/shard_map/ppermute | solution.py:284
  49.8 4.7 %collective-permute-start.18 = (bf16[96,128]{1,0:T(8,128)(2,1)S(1)}, bf16[96,128]{1,0:T(8,128)(2,1)S(1)}, u32[]{:S(2)}, u32[]{:S(2)}) collective-permute-start(bf16[96,128]{1,0:T(8,128)(2,1)S(1)} %shard_map.75.refs_0_), channel_id=1, source_target_pairs={{0,16},{8,24},{16,0},{24,8},{1,17},{9,25},{17,1},{25,9},{2,18},{10... | collective-permute-start | bytes 73736 | tf_op jit(solution)/shard_map/ppermute | solution.py:284
  50.4 4.1 %collective-permute-start.17 = (bf16[96,128]{1,0:T(8,128)(2,1)S(1)}, bf16[96,128]{1,0:T(8,128)(2,1)S(1)}, u32[]{:S(2)}, u32[]{:S(2)}) collective-permute-start(bf16[96,128]{1,0:T(8,128)(2,1)S(1)} %shard_map.75.refs_0_), channel_id=1, source_target_pairs={{0,8},{8,16},{16,24},{24,0},{1,9},{9,17},{17,25},{25,1},{2,10},{10... | collective-permute-start | bytes 73736 | tf_op jit(solution)/shard_map/ppermute | solution.py:284
where the time goes:
time: 59.1 us; the launch traced here: 58.1 us
  starting transfers between devices  29.6 us (50%)
  Pallas kernels  19.2 us (32%)
  waiting for transfers between devices  7.57 us (13%)
  local copies, waits for them, and re-layouts  0.91 us (2%)
  between operations  0.82 us (1%)
    ppermute x14, starting transfers between devices, send(): return lax.ppermute(x, 'feat', pairs)  25.9 us
    pallas_call x9, Pallas kernels, call(): pl.pallas_call(kernel, in_specs=in_specs, out_specs=out_specs, out_shape=...  19.2 us
    ppermute x14, waiting for transfers between devices, send(): return lax.ppermute(x, 'feat', pairs)  7.55 us
    ppermute x6, starting transfers between devices, exchange(): parts.append(lax.ppermute(value, 'layer', pairs))  3.65 us
  transfers between devices with their start and end apart: 20, of which 5 were waited for; matrix products, arithmetic and copies ran while one was open for 0% of the time, Pallas kernels for 27%

commit v1 on v0

--- a/solution.py
+++ b/solution.py
@@ -13,6 +13,19 @@
 SUB = 8
 F32 = jnp.float32
 BF16 = jnp.bfloat16
+
+
+def lanes_of(x, index):
+    numbers = lax.GatherDimensionNumbers(
+        offset_dims=(),
+        collapsed_slice_dims=(1,),
+        start_index_map=(1,),
+        operand_batching_dims=(0,),
+        start_indices_batching_dims=(0,),
+    )
+    return lax.gather(
+        x, index[..., None], numbers, slice_sizes=(1, 1), mode=lax.GatherScatterMode.PROMISE_IN_BOUNDS
+    )
 
 
 def pack_kernel(starts, chosen, tgt, held):
@@ -59,9 +72,7 @@
         for h in range(blocks):
             for q in groups:
                 t = (q - groups[0]) * quarter + m * SUB
-                got = jnp.take_along_axis(
-                    dense[t : t + SUB, h * LANES : (h + 1) * LANES], low, axis=1
-                )
+                got = lanes_of(dense[t : t + SUB, h * LANES : (h + 1) * LANES], low)
                 value = jnp.where(key == (first_block + h) * per + q, got, value)
         picked.append(value)
     return picked
@@ -76,7 +87,7 @@
         parts = []
         for h in range(size // LANES):
             at = inv[t : t + SUB, first + h * LANES : first + (h + 1) * LANES]
-            got = jnp.take_along_axis(source, jnp.bitwise_and(at, LANES - 1), axis=1)
+            got = lanes_of(source, jnp.bitwise_and(at, LANES - 1))
             parts.append(jnp.where(at >= 0, got, 0.0))
         rows_out.append(jnp.concatenate(parts, axis=1))
     return jnp.concatenate(rows_out, axis=0)
@@ -280,7 +291,7 @@
     def exchange(value):
         parts = [value]
         for s in range(1, n_layer):
-            pairs = [(d, (d + s) % n_layer) for d in range(n_layer)]
+            pairs = [(d, partner(d, s, n_layer)) for d in range(n_layer)]
             parts.append(lax.ppermute(value, "layer", pairs))
         return parts
 
@@ -312,22 +323,26 @@
         ]
     grad_parts = exchange(vals[0])
 
-    def out_scratch(rows, columns):
+    def out_scratch(rows, columns, block):
         return [pltpu.VMEM((rows, columns), BF16), pltpu.SemaphoreType.DMA((feat_dev // block,))]
 
     args = (*e, *pre_parts, *inv, squares)
     dec_grad = call(
-        functools.partial(dec_grad_kernel, feat, n_layer, block, tokens * width),
+        functools.partial(dec_grad_kernel, feat, n_layer, LANES, tokens * width),
         args, [VMEM] * len(args), ANY, shape((1, feat_dev, width), BF16),
-        out_scratch(feat_dev, width), 2 * half_flops, 2 * feat_dev * width,
+        out_scratch(feat_dev, width, LANES), 2 * half_flops, 2 * feat_dev * width,
     )
     args = (*grad_parts, turned, *inv)
     enc_grad = call(
         functools.partial(enc_grad_kernel, n_layer, block, min(512, width)),
         args, [VMEM] * len(args), ANY, shape((1, width, feat_dev), BF16),
-        out_scratch(width, feat_dev), 2 * half_flops, 2 * feat_dev * width,
+        out_scratch(width, feat_dev, block), 2 * half_flops, 2 * feat_dev * width,
     )
     return (dec_grad, enc_grad)
+
+
+def partner(d, s, count):
+    return d ^ s if count & (count - 1) == 0 else (d + s) % count
 
 
 def steps_of(outer):

time: 59.1 us -> 58.1 us (0.983); the launches traced: 58.1 us -> 57.9 us
  transfers between devices with their start and end apart: 20 -> 20, of which waited for: 5 -> 5; matrix products, arithmetic and copies ran while one was open for 0% -> 0% of each run, Pallas kernels for 27% -> 26%
where the time goes in v1:
time: 58.1 us; the launch traced here: 57.9 us
  starting transfers between devices  29.8 us (51%)
  Pallas kernels  18.9 us (33%)
  waiting for transfers between devices  7.43 us (13%)
  local copies, waits for them, and re-layouts  0.91 us (2%)
  between operations  0.82 us (1%)
    ppermute x14, starting transfers between devices, send(): return lax.ppermute(x, 'feat', pairs)  25.9 us
    pallas_call x9, Pallas kernels, call(): pl.pallas_call(kernel, in_specs=in_specs, out_specs=out_specs, out_shape=...  18.9 us
    ppermute x14, waiting for transfers between devices, send(): return lax.ppermute(x, 'feat', pairs)  7.42 us
    ppermute x6, starting transfers between devices, exchange(): parts.append(lax.ppermute(value, 'layer', pairs))  3.91 us
  transfers between devices with their start and end apart: 20, of which 5 were waited for; matrix products, arithmetic and copies ran while one was open for 0% of the time, Pallas kernels for 26%

profile of v1, /device:TPU:0, one launch (start us, length us, event | category | flops | bytes accessed | tf_op | source)
XLA Modules:
  0.0 57.9 jit_solution(17054325769139510849)
XLA Ops:
  0.6 3.1 %collective-permute-start.8 = (bf16[1,48,2048]{2,1,0:T(8,128)(2,1)}, bf16[1,48,2048]{2,1,0:T(8,128)(2,1)S(1)}, u32[]{:S(2)}, u32[]{:S(2)}) collective-permute-start(bf16[1,48,2048]{2,1,0:T(8,128)(2,1)} %refs_0_.5), channel_id=1, source_target_pairs={{0,2},{1,3},{2,4},{3,5},{4,6},{5,7},{6,0},{7,1},{8,10},{9,11},{10,... | collective-permute-start | bytes 589832 | tf_op jit(solution)/shard_map/ppermute | solution.py:238
  3.7 2.1 %collective-permute-start.12 = (bf16[1,48,2048]{2,1,0:T(8,128)(2,1)}, bf16[1,48,2048]{2,1,0:T(8,128)(2,1)S(1)}, u32[]{:S(2)}, u32[]{:S(2)}) collective-permute-start(bf16[1,48,2048]{2,1,0:T(8,128)(2,1)} %refs_0_.5), channel_id=1, source_target_pairs={{0,6},{1,7},{2,0},{3,1},{4,2},{5,3},{6,4},{7,5},{8,14},{9,15},{10,... | collective-permute-start | bytes 589832 | tf_op jit(solution)/shard_map/ppermute | solution.py:238
  5.8 1.6 %collective-permute-start.7 = (bf16[1,48,2048]{2,1,0:T(8,128)(2,1)}, bf16[1,48,2048]{2,1,0:T(8,128)(2,1)S(1)}, u32[]{:S(2)}, u32[]{:S(2)}) collective-permute-start(bf16[1,48,2048]{2,1,0:T(8,128)(2,1)} %refs_0_.5), channel_id=1, source_target_pairs={{0,1},{1,0},{2,3},{3,2},{4,5},{5,4},{6,7},{7,6},{8,9},{9,8},{10,11... | collective-permute-start | bytes 589832 | tf_op jit(solution)/shard_map/ppermute | solution.py:238
  7.5 1.8 %collective-permute-start.5 = (bf16[1,48,2048]{2,1,0:T(8,128)(2,1)}, bf16[1,48,2048]{2,1,0:T(8,128)(2,1)S(1)}, u32[]{:S(2)}, u32[]{:S(2)}) collective-permute-start(bf16[1,48,2048]{2,1,0:T(8,128)(2,1)} %refs_0_.7), channel_id=1, source_target_pairs={{0,6},{1,7},{2,0},{3,1},{4,2},{5,3},{6,4},{7,5},{8,14},{9,15},{10,... | collective-permute-start | bytes 589832 | tf_op jit(solution)/shard_map/ppermute | solution.py:238
  9.6 0.8 %copy-done.3 = s32[384,32]{0,1:T(8,128)S(1)} copy-done((s32[384,32]{0,1:T(8,128)S(1)}, s32[384,32]{0,1:T(8,128)}, u32[]{:S(2)}) %copy-start.3) | copy-done | bytes 49176
  10.4 0.8 %shard_map.68.refs_9_.tgt.refs_5_ = s32[96,128]{1,0:T(8,128)S(1)} custom-call(s32[9]{0:T(128)S(1)} %stack.39.starts, s32[32,384]{1,0:T(8,128)S(1)} %bitcast.10), custom_call_target="tpu_custom_call" | custom-call | flops 12288 | bytes 196608 | tf_op jit(solution)/shard_map/pallas_call | solution.py:208
  11.2 0.6 collective-permute-done.8.refs_2_
  11.8 6.8 %collective-permute-start.10 = (bf16[1,48,2048]{2,1,0:T(8,128)(2,1)S(1)}, bf16[1,48,2048]{2,1,0:T(8,128)(2,1)S(1)}, u32[]{:S(2)}, u32[]{:S(2)}) collective-permute-start(bf16[1,48,2048]{2,1,0:T(8,128)(2,1)S(1)} %collective-permute-done.8.refs_2_), channel_id=1, source_target_pairs={{0,2},{1,3},{2,4},{3,5},{4,6},{5,7},{6,0},{7,1},{8,10},{9,11},{10,... | collective-permute-start | bytes 589832 | tf_op jit(solution)/shard_map/ppermute | solution.py:238
  18.6 2.5 %shard_map.71.refs_13_.refs_6_ = s32[192,1024]{1,0:T(8,128)S(1)} custom-call(s32[96,128]{1,0:T(8,128)S(1)} %shard_map.68.refs_9_.tgt.refs_5_), custom_call_target="tpu_custom_call" | custom-call | flops 6442450944 | bytes 786432 | tf_op jit(solution)/shard_map/pallas_call | solution.py:208
  21.1 1.9 %collective-permute-start = (bf16[1,48,2048]{2,1,0:T(8,128)(2,1)S(1)}, bf16[1,48,2048]{2,1,0:T(8,128)(2,1)S(1)}, u32[]{:S(2)}, u32[]{:S(2)}) collective-permute-start(bf16[1,48,2048]{2,1,0:T(8,128)(2,1)S(1)} %copy-done.1), channel_id=1, source_target_pairs={{0,1},{1,0},{2,3},{3,2},{4,5},{5,4},{6,7},{7,6},{8,9},{9,8},{10,11... | collective-permute-start | bytes 589832 | tf_op jit(solution)/shard_map/ppermute | solution.py:238
  23.2 1.8 %collective-permute-start.13 = (bf16[1,48,2048]{2,1,0:T(8,128)(2,1)S(1)}, bf16[1,48,2048]{2,1,0:T(8,128)(2,1)S(1)}, u32[]{:S(2)}, u32[]{:S(2)}) collective-permute-start(bf16[1,48,2048]{2,1,0:T(8,128)(2,1)S(1)} %collective-permute-done.12.refs_6_), channel_id=1, source_target_pairs={{0,1},{1,0},{2,3},{3,2},{4,5},{5,4},{6,7},{7,6},{8,9},{9,8},{10,11... | collective-permute-start | bytes 589832 | tf_op jit(solution)/shard_map/ppermute | solution.py:238
  25.0 1.1 %collective-permute-start.2 = (bf16[1,48,2048]{2,1,0:T(8,128)(2,1)S(1)}, bf16[1,48,2048]{2,1,0:T(8,128)(2,1)S(1)}, u32[]{:S(2)}, u32[]{:S(2)}) collective-permute-start(bf16[1,48,2048]{2,1,0:T(8,128)(2,1)S(1)} %collective-permute-done.1.refs_2_), channel_id=1, source_target_pairs={{0,1},{1,0},{2,3},{3,2},{4,5},{5,4},{6,7},{7,6},{8,9},{9,8},{10,11... | collective-permute-start | bytes 589832 | tf_op jit(solution)/shard_map/ppermute | solution.py:238
  26.1 1.7 %collective-permute-done.10.refs_4_ = bf16[1,48,2048]{2,1,0:T(8,128)(2,1)S(1)} collective-permute-done((bf16[1,48,2048]{2,1,0:T(8,128)(2,1)S(1)}, bf16[1,48,2048]{2,1,0:T(8,128)(2,1)S(1)}, u32[]{:S(2)}, u32[]{:S(2)}) %collective-permute-start.10) | collective-permute-done | bytes 196640 | tf_op jit(solution)/shard_map/ppermute | solution.py:238
  27.8 1.5 %collective-permute-start.11 = (bf16[1,48,2048]{2,1,0:T(8,128)(2,1)S(1)}, bf16[1,48,2048]{2,1,0:T(8,128)(2,1)S(1)}, u32[]{:S(2)}, u32[]{:S(2)}) collective-permute-start(bf16[1,48,2048]{2,1,0:T(8,128)(2,1)S(1)} %collective-permute-done.10.refs_4_), channel_id=1, source_target_pairs={{0,1},{1,0},{2,3},{3,2},{4,5},{5,4},{6,7},{7,6},{8,9},{9,8},{10,11... | collective-permute-start | bytes 589832 | tf_op jit(solution)/shard_map/ppermute | solution.py:238
  29.3 2.5 %shard_map.70.refs_12_.refs_5_ = s32[192,1024]{1,0:T(8,128)S(1)} custom-call(s32[96,128]{1,0:T(8,128)S(1)} %shard_map.68.refs_9_.tgt.refs_5_), custom_call_target="tpu_custom_call" | custom-call | flops 6442450944 | bytes 786432 | tf_op jit(solution)/shard_map/pallas_call | solution.py:208
  31.8 0.7 %collective-permute-start.3 = (bf16[1,48,2048]{2,1,0:T(8,128)(2,1)S(1)}, bf16[1,48,2048]{2,1,0:T(8,128)(2,1)S(1)}, u32[]{:S(2)}, u32[]{:S(2)}) collective-permute-start(bf16[1,48,2048]{2,1,0:T(8,128)(2,1)S(1)} %collective-permute-done.1.refs_2_), channel_id=1, source_target_pairs={{0,2},{1,3},{2,4},{3,5},{4,6},{5,7},{6,0},{7,1},{8,10},{9,11},{10,... | collective-permute-start | bytes 589832 | tf_op jit(solution)/shard_map/ppermute | solution.py:238
  32.5 4.3 %collective-permute-done.13.refs_7_ = bf16[1,48,2048]{2,1,0:T(8,128)(2,1)S(1)} collective-permute-done((bf16[1,48,2048]{2,1,0:T(8,128)(2,1)S(1)}, bf16[1,48,2048]{2,1,0:T(8,128)(2,1)S(1)}, u32[]{:S(2)}, u32[]{:S(2)}) %collective-permute-start.13) | collective-permute-done | bytes 196640 | tf_op jit(solution)/shard_map/ppermute | solution.py:238
  36.7 2.3 %collective-permute-start.6 = (bf16[1,48,2048]{2,1,0:T(8,128)(2,1)S(1)}, bf16[1,48,2048]{2,1,0:T(8,128)(2,1)S(1)}, u32[]{:S(2)}, u32[]{:S(2)}) collective-permute-start(bf16[1,48,2048]{2,1,0:T(8,128)(2,1)S(1)} %collective-permute-done.5.refs_6_.refs_2_), channel_id=1, source_target_pairs={{0,1},{1,0},{2,3},{3,2},{4,5},{5,4},{6,7},{7,6},{8,9},{9,8},{10,11... | collective-permute-start | bytes 589832 | tf_op jit(solution)/shard_map/ppermute | solution.py:238
  39.1 0.4 collective-permute-done.2.refs_3_
  39.5 0.8 %collective-permute-start.4 = (bf16[1,48,2048]{2,1,0:T(8,128)(2,1)S(1)}, bf16[1,48,2048]{2,1,0:T(8,128)(2,1)S(1)}, u32[]{:S(2)}, u32[]{:S(2)}) collective-permute-start(bf16[1,48,2048]{2,1,0:T(8,128)(2,1)S(1)} %collective-permute-done.2.refs_3_), channel_id=1, source_target_pairs={{0,2},{1,3},{2,4},{3,5},{4,6},{5,7},{6,0},{7,1},{8,10},{9,11},{10,... | collective-permute-start | bytes 589832 | tf_op jit(solution)/shard_map/ppermute | solution.py:238
  40.3 1.7 %shard_map.74.refs_6_ = f32[96,128]{1,0:T(8,128)S(1)} custom-call(bf16[1,48,2048]{2,1,0:T(8,128)(2,1)S(1)} %copy-done.1, bf16[1,48,2048]{2,1,0:T(8,128)(2,1)S(1)} %collective-permute-done.refs_1_, bf16[1,48,2048]{2,1,0:T(8,128)(2,1)S(1)} %collective-permute-done.1.refs_2_, bf16[1,48,2048]{2,1,0:T(8,128)(2,1)S(1)} %collective-permute-done.2.refs_3_, ...), custom_call_target="tpu_custom_call" | custom-call | flops 805306368 | bytes 786432 | tf_op jit(solution)/shard_map/pallas_call | solution.py:208
  42.0 2.0 %shard_map.69.refs_8_ = bf16[96,128]{1,0:T(8,128)(2,1)S(1)} custom-call(bf16[1,48,2048]{2,1,0:T(8,128)(2,1)S(1)} %copy-done.2, bf16[1,48,2048]{2,1,0:T(8,128)(2,1)S(1)} %collective-permute-done.7.refs_1_, bf16[1,48,2048]{2,1,0:T(8,128)(2,1)S(1)} %collective-permute-done.8.refs_2_, bf16[1,48,2048]{2,1,0:T(8,128)(2,1)S(1)} %collective-permute-done.9.refs_3_, ...), custom_call_target="tpu_custom_call" | custom-call | flops 1610612736 | bytes 1572864 | tf_op jit(solution)/shard_map/pallas_call | solution.py:208
  44.1 1.6 %collective-permute-start.15 = (bf16[96,128]{1,0:T(8,128)(2,1)S(1)}, bf16[96,128]{1,0:T(8,128)(2,1)S(1)}, u32[]{:S(2)}, u32[]{:S(2)}) collective-permute-start(bf16[96,128]{1,0:T(8,128)(2,1)S(1)} %shard_map.69.refs_8_), channel_id=1, source_target_pairs={{0,16},{8,24},{16,0},{24,8},{1,17},{9,25},{17,1},{25,9},{2,18},{10... | collective-permute-start | bytes 73736 | tf_op jit(solution)/shard_map/ppermute | solution.py:295
  45.7 0.5 shard_map.72
  46.2 0.3 collective-permute-start.14
  46.5 0.5 collective-permute-done.4.refs_5_.refs_1_
  47.0 1.7 %shard_map.75.refs_0_ = bf16[96,128]{1,0:T(8,128)(2,1)S(1)} custom-call(bf16[1,48,2048]{2,1,0:T(8,128)(2,1)S(1)} %collective-permute-done.3.refs_4_.refs_0_, bf16[1,48,2048]{2,1,0:T(8,128)(2,1)S(1)} %collective-permute-done.4.refs_5_.refs_1_, bf16[1,48,2048]{2,1,0:T(8,128)(2,1)S(1)} %collective-permute-done.5.refs_6_.refs_2_, ...), custom_call_target="tpu_custom_call" | custom-call | flops 805306368 | bytes 786432 | tf_op jit(solution)/shard_map/pallas_call | solution.py:208
  48.7 0.7 %collective-permute-start.19 = (bf16[96,128]{1,0:T(8,128)(2,1)S(1)}, bf16[96,128]{1,0:T(8,128)(2,1)S(1)}, u32[]{:S(2)}, u32[]{:S(2)}) collective-permute-start(bf16[96,128]{1,0:T(8,128)(2,1)S(1)} %shard_map.75.refs_0_), channel_id=1, source_target_pairs={{0,24},{8,16},{16,8},{24,0},{1,25},{9,17},{17,9},{25,1},{2,26},{10... | collective-permute-start | bytes 73736 | tf_op jit(solution)/shard_map/ppermute | solution.py:295
  49.5 0.9 %collective-permute-start.18 = (bf16[96,128]{1,0:T(8,128)(2,1)S(1)}, bf16[96,128]{1,0:T(8,128)(2,1)S(1)}, u32[]{:S(2)}, u32[]{:S(2)}) collective-permute-start(bf16[96,128]{1,0:T(8,128)(2,1)S(1)} %shard_map.75.refs_0_), channel_id=1, source_target_pairs={{0,16},{8,24},{16,0},{24,8},{1,17},{9,25},{17,1},{25,9},{2,18},{10... | collective-permute-start | bytes 73736 | tf_op jit(solution)/shard_map/ppermute | solution.py:295
  50.4 0.3 collective-permute-start.17
  50.7 3.6 %shard_map.73 = bf16[1,1024,2048]{2,1,0:T(8,128)(2,1)} custom-call(bf16[1,48,2048]{2,1,0:T(8,128)(2,1)S(1)} %copy-done.1, bf16[1,48,2048]{2,1,0:T(8,128)(2,1)S(1)} %collective-permute-done.refs_1_, bf16[1,48,2048]{2,1,0:T(8,128)(2,1)S(1)} %collective-permute-done.1.refs_2_, bf16[1,48,2048]{2,1,0:T(8,128)(2,1)S(1)} %collective-permute-done.2.refs_3_, ...), custom_call_target="tpu_custom_call" | custom-call | flops 1610612736 | bytes 4194304 | tf_op jit(solution)/shard_map/pallas_call | solution.py:208
  54.3 3.6 %shard_map.76 = bf16[1,2048,1024]{2,1,0:T(8,128)(2,1)} custom-call(bf16[96,128]{1,0:T(8,128)(2,1)S(1)} %shard_map.75.refs_0_, bf16[96,128]{1,0:T(8,128)(2,1)S(1)} %collective-permute-done.17.refs_1_, bf16[96,128]{1,0:T(8,128)(2,1)S(1)} %collective-permute-done.18.refs_2_, bf16[96,128]{1,0:T(8,128)(2,1)S(1)} %collective-permute-done.19.refs_3_, ...), custom_call_target="tpu_custom_call" | custom-call | flops 1610612736 | bytes 4194304 | tf_op jit(solution)/shard_map/pallas_call | solution.py:208
  (28 shorter events, 0.7 us)
Async XLA Ops:
  0.6 11.1 %collective-permute-start.8 = (bf16[1,48,2048]{2,1,0:T(8,128)(2,1)}, bf16[1,48,2048]{2,1,0:T(8,128)(2,1)S(1)}, u32[]{:S(2)}, u32[]{:S(2)}) collective-permute-start(bf16[1,48,2048]{2,1,0:T(8,128)(2,1)} %refs_0_.5), channel_id=1, source_target_pairs={{0,2},{1,3},{2,4},{3,5},{4,6},{5,7},{6,0},{7,1},{8,10},{9,11},{10,... | collective-permute-start | bytes 589832 | tf_op jit(solution)/shard_map/ppermute | solution.py:238
  3.7 17.4 %collective-permute-start.12 = (bf16[1,48,2048]{2,1,0:T(8,128)(2,1)}, bf16[1,48,2048]{2,1,0:T(8,128)(2,1)S(1)}, u32[]{:S(2)}, u32[]{:S(2)}) collective-permute-start(bf16[1,48,2048]{2,1,0:T(8,128)(2,1)} %refs_0_.5), channel_id=1, source_target_pairs={{0,6},{1,7},{2,0},{3,1},{4,2},{5,3},{6,4},{7,5},{8,14},{9,15},{10,... | collective-permute-start | bytes 589832 | tf_op jit(solution)/shard_map/ppermute | solution.py:238
  5.8 17.2 %collective-permute-start.7 = (bf16[1,48,2048]{2,1,0:T(8,128)(2,1)}, bf16[1,48,2048]{2,1,0:T(8,128)(2,1)S(1)}, u32[]{:S(2)}, u32[]{:S(2)}) collective-permute-start(bf16[1,48,2048]{2,1,0:T(8,128)(2,1)} %refs_0_.5), channel_id=1, source_target_pairs={{0,1},{1,0},{2,3},{3,2},{4,5},{5,4},{6,7},{7,6},{8,9},{9,8},{10,11... | collective-permute-start | bytes 589832 | tf_op jit(solution)/shard_map/ppermute | solution.py:238
  7.5 15.8 %collective-permute-start.5 = (bf16[1,48,2048]{2,1,0:T(8,128)(2,1)}, bf16[1,48,2048]{2,1,0:T(8,128)(2,1)S(1)}, u32[]{:S(2)}, u32[]{:S(2)}) collective-permute-start(bf16[1,48,2048]{2,1,0:T(8,128)(2,1)} %refs_0_.7), channel_id=1, source_target_pairs={{0,6},{1,7},{2,0},{3,1},{4,2},{5,3},{6,4},{7,5},{8,14},{9,15},{10,... | collective-permute-start | bytes 589832 | tf_op jit(solution)/shard_map/ppermute | solution.py:238
  9.3 15.8 %collective-permute-start.1 = (bf16[1,48,2048]{2,1,0:T(8,128)(2,1)}, bf16[1,48,2048]{2,1,0:T(8,128)(2,1)S(1)}, u32[]{:S(2)}, u32[]{:S(2)}) collective-permute-start(bf16[1,48,2048]{2,1,0:T(8,128)(2,1)} %refs_0_.7), channel_id=1, source_target_pairs={{0,2},{1,3},{2,4},{3,5},{4,6},{5,7},{6,0},{7,1},{8,10},{9,11},{10,... | collective-permute-start | bytes 589832 | tf_op jit(solution)/shard_map/ppermute | solution.py:238
  9.6 0.8 %copy-start.3 = (s32[384,32]{0,1:T(8,128)S(1)}, s32[384,32]{0,1:T(8,128)}, u32[]{:S(2)}) copy-start(s32[384,32]{0,1:T(8,128)} %param.9) | copy-start | bytes 147460
  11.2 9.9 %copy-start.1 = (bf16[1,48,2048]{2,1,0:T(8,128)(2,1)S(1)}, bf16[1,48,2048]{2,1,0:T(8,128)(2,1)}, u32[]{:S(2)}) copy-start(bf16[1,48,2048]{2,1,0:T(8,128)(2,1)} %refs_0_.7) | copy-start | bytes 589828
  11.8 16.0 %collective-permute-start.10 = (bf16[1,48,2048]{2,1,0:T(8,128)(2,1)S(1)}, bf16[1,48,2048]{2,1,0:T(8,128)(2,1)S(1)}, u32[]{:S(2)}, u32[]{:S(2)}) collective-permute-start(bf16[1,48,2048]{2,1,0:T(8,128)(2,1)S(1)} %collective-permute-done.8.refs_2_), channel_id=1, source_target_pairs={{0,2},{1,3},{2,4},{3,5},{4,6},{5,7},{6,0},{7,1},{8,10},{9,11},{10,... | collective-permute-start | bytes 589832 | tf_op jit(solution)/shard_map/ppermute | solution.py:238
  21.1 19.2 %copy-start = (bf16[1,1024,2048]{2,1,0:T(8,128)(2,1)S(1)}, bf16[1,1024,2048]{2,1,0:T(8,128)(2,1)}, u32[]{:S(2)}) copy-start(bf16[1,1024,2048]{2,1,0:T(8,128)(2,1)} %refs_4_.3) | copy-start | bytes 12582916
  21.1 10.7 %collective-permute-start = (bf16[1,48,2048]{2,1,0:T(8,128)(2,1)S(1)}, bf16[1,48,2048]{2,1,0:T(8,128)(2,1)S(1)}, u32[]{:S(2)}, u32[]{:S(2)}) collective-permute-start(bf16[1,48,2048]{2,1,0:T(8,128)(2,1)S(1)} %copy-done.1), channel_id=1, source_target_pairs={{0,1},{1,0},{2,3},{3,2},{4,5},{5,4},{6,7},{7,6},{8,9},{9,8},{10,11... | collective-permute-start | bytes 589832 | tf_op jit(solution)/shard_map/ppermute | solution.py:238
  23.0 19.0 %collective-permute-start.9 = (bf16[1,48,2048]{2,1,0:T(8,128)(2,1)S(1)}, bf16[1,48,2048]{2,1,0:T(8,128)(2,1)S(1)}, u32[]{:S(2)}, u32[]{:S(2)}) collective-permute-start(bf16[1,48,2048]{2,1,0:T(8,128)(2,1)S(1)} %collective-permute-done.8.refs_2_), channel_id=1, source_target_pairs={{0,1},{1,0},{2,3},{3,2},{4,5},{5,4},{6,7},{7,6},{8,9},{9,8},{10,11... | collective-permute-start | bytes 589832 | tf_op jit(solution)/shard_map/ppermute | solution.py:238
  23.2 13.5 %collective-permute-start.13 = (bf16[1,48,2048]{2,1,0:T(8,128)(2,1)S(1)}, bf16[1,48,2048]{2,1,0:T(8,128)(2,1)S(1)}, u32[]{:S(2)}, u32[]{:S(2)}) collective-permute-start(bf16[1,48,2048]{2,1,0:T(8,128)(2,1)S(1)} %collective-permute-done.12.refs_6_), channel_id=1, source_target_pairs={{0,1},{1,0},{2,3},{3,2},{4,5},{5,4},{6,7},{7,6},{8,9},{9,8},{10,11... | collective-permute-start | bytes 589832 | tf_op jit(solution)/shard_map/ppermute | solution.py:238
  25.0 14.5 %collective-permute-start.2 = (bf16[1,48,2048]{2,1,0:T(8,128)(2,1)S(1)}, bf16[1,48,2048]{2,1,0:T(8,128)(2,1)S(1)}, u32[]{:S(2)}, u32[]{:S(2)}) collective-permute-start(bf16[1,48,2048]{2,1,0:T(8,128)(2,1)S(1)} %collective-permute-done.1.refs_2_), channel_id=1, source_target_pairs={{0,1},{1,0},{2,3},{3,2},{4,5},{5,4},{6,7},{7,6},{8,9},{9,8},{10,11... | collective-permute-start | bytes 589832 | tf_op jit(solution)/shard_map/ppermute | solution.py:238
  27.8 14.2 %collective-permute-start.11 = (bf16[1,48,2048]{2,1,0:T(8,128)(2,1)S(1)}, bf16[1,48,2048]{2,1,0:T(8,128)(2,1)S(1)}, u32[]{:S(2)}, u32[]{:S(2)}) collective-permute-start(bf16[1,48,2048]{2,1,0:T(8,128)(2,1)S(1)} %collective-permute-done.10.refs_4_), channel_id=1, source_target_pairs={{0,1},{1,0},{2,3},{3,2},{4,5},{5,4},{6,7},{7,6},{8,9},{9,8},{10,11... | collective-permute-start | bytes 589832 | tf_op jit(solution)/shard_map/ppermute | solution.py:238
  31.8 10.3 %copy-start.2 = (bf16[1,48,2048]{2,1,0:T(8,128)(2,1)S(1)}, bf16[1,48,2048]{2,1,0:T(8,128)(2,1)}, u32[]{:S(2)}) copy-start(bf16[1,48,2048]{2,1,0:T(8,128)(2,1)} %refs_0_.5) | copy-start | bytes 589828
  31.8 10.3 %copy-start.4 = (bf16[1,2048,1024]{2,1,0:T(8,128)(2,1)S(1)}, bf16[1,2048,1024]{2,1,0:T(8,128)(2,1)}, u32[]{:S(2)}) copy-start(bf16[1,2048,1024]{2,1,0:T(8,128)(2,1)} %refs_8_.1) | copy-start | bytes 12582916
  31.8 14.7 %collective-permute-start.3 = (bf16[1,48,2048]{2,1,0:T(8,128)(2,1)S(1)}, bf16[1,48,2048]{2,1,0:T(8,128)(2,1)S(1)}, u32[]{:S(2)}, u32[]{:S(2)}) collective-permute-start(bf16[1,48,2048]{2,1,0:T(8,128)(2,1)S(1)} %collective-permute-done.1.refs_2_), channel_id=1, source_target_pairs={{0,2},{1,3},{2,4},{3,5},{4,6},{5,7},{6,0},{7,1},{8,10},{9,11},{10,... | collective-permute-start | bytes 589832 | tf_op jit(solution)/shard_map/ppermute | solution.py:238
  36.7 9.4 %collective-permute-start.6 = (bf16[1,48,2048]{2,1,0:T(8,128)(2,1)S(1)}, bf16[1,48,2048]{2,1,0:T(8,128)(2,1)S(1)}, u32[]{:S(2)}, u32[]{:S(2)}) collective-permute-start(bf16[1,48,2048]{2,1,0:T(8,128)(2,1)S(1)} %collective-permute-done.5.refs_6_.refs_2_), channel_id=1, source_target_pairs={{0,1},{1,0},{2,3},{3,2},{4,5},{5,4},{6,7},{7,6},{8,9},{9,8},{10,11... | collective-permute-start | bytes 589832 | tf_op jit(solution)/shard_map/ppermute | solution.py:238
  39.5 7.5 %collective-permute-start.4 = (bf16[1,48,2048]{2,1,0:T(8,128)(2,1)S(1)}, bf16[1,48,2048]{2,1,0:T(8,128)(2,1)S(1)}, u32[]{:S(2)}, u32[]{:S(2)}) collective-permute-start(bf16[1,48,2048]{2,1,0:T(8,128)(2,1)S(1)} %collective-permute-done.2.refs_3_), channel_id=1, source_target_pairs={{0,2},{1,3},{2,4},{3,5},{4,6},{5,7},{6,0},{7,1},{8,10},{9,11},{10,... | collective-permute-start | bytes 589832 | tf_op jit(solution)/shard_map/ppermute | solution.py:238
  44.0 6.4 %collective-permute-start.16 = (bf16[96,128]{1,0:T(8,128)(2,1)S(1)}, bf16[96,128]{1,0:T(8,128)(2,1)S(1)}, u32[]{:S(2)}, u32[]{:S(2)}) collective-permute-start(bf16[96,128]{1,0:T(8,128)(2,1)S(1)} %shard_map.69.refs_8_), channel_id=1, source_target_pairs={{0,24},{8,16},{16,8},{24,0},{1,25},{9,17},{17,9},{25,1},{2,26},{10... | collective-permute-start | bytes 73736 | tf_op jit(solution)/shard_map/ppermute | solution.py:295
  44.1 6.6 %collective-permute-start.15 = (bf16[96,128]{1,0:T(8,128)(2,1)S(1)}, bf16[96,128]{1,0:T(8,128)(2,1)S(1)}, u32[]{:S(2)}, u32[]{:S(2)}) collective-permute-start(bf16[96,128]{1,0:T(8,128)(2,1)S(1)} %shard_map.69.refs_8_), channel_id=1, source_target_pairs={{0,16},{8,24},{16,0},{24,8},{1,17},{9,25},{17,1},{25,9},{2,18},{10... | collective-permute-start | bytes 73736 | tf_op jit(solution)/shard_map/ppermute | solution.py:295
  46.2 4.5 %collective-permute-start.14 = (bf16[96,128]{1,0:T(8,128)(2,1)S(1)}, bf16[96,128]{1,0:T(8,128)(2,1)S(1)}, u32[]{:S(2)}, u32[]{:S(2)}) collective-permute-start(bf16[96,128]{1,0:T(8,128)(2,1)S(1)} %shard_map.69.refs_8_), channel_id=1, source_target_pairs={{0,8},{8,0},{16,24},{24,16},{1,9},{9,1},{17,25},{25,17},{2,10},{10... | collective-permute-start | bytes 73736 | tf_op jit(solution)/shard_map/ppermute | solution.py:295
  48.7 5.6 %collective-permute-start.19 = (bf16[96,128]{1,0:T(8,128)(2,1)S(1)}, bf16[96,128]{1,0:T(8,128)(2,1)S(1)}, u32[]{:S(2)}, u32[]{:S(2)}) collective-permute-start(bf16[96,128]{1,0:T(8,128)(2,1)S(1)} %shard_map.75.refs_0_), channel_id=1, source_target_pairs={{0,24},{8,16},{16,8},{24,0},{1,25},{9,17},{17,9},{25,1},{2,26},{10... | collective-permute-start | bytes 73736 | tf_op jit(solution)/shard_map/ppermute | solution.py:295
  49.5 4.8 %collective-permute-start.18 = (bf16[96,128]{1,0:T(8,128)(2,1)S(1)}, bf16[96,128]{1,0:T(8,128)(2,1)S(1)}, u32[]{:S(2)}, u32[]{:S(2)}) collective-permute-start(bf16[96,128]{1,0:T(8,128)(2,1)S(1)} %shard_map.75.refs_0_), channel_id=1, source_target_pairs={{0,16},{8,24},{16,0},{24,8},{1,17},{9,25},{17,1},{25,9},{2,18},{10... | collective-permute-start | bytes 73736 | tf_op jit(solution)/shard_map/ppermute | solution.py:295
  50.4 3.9 %collective-permute-start.17 = (bf16[96,128]{1,0:T(8,128)(2,1)S(1)}, bf16[96,128]{1,0:T(8,128)(2,1)S(1)}, u32[]{:S(2)}, u32[]{:S(2)}) collective-permute-start(bf16[96,128]{1,0:T(8,128)(2,1)S(1)} %shard_map.75.refs_0_), channel_id=1, source_target_pairs={{0,8},{8,0},{16,24},{24,16},{1,9},{9,1},{17,25},{25,17},{2,10},{10... | collective-permute-start | bytes 73736 | tf_op jit(solution)/shard_map/ppermute | solution.py:295

commit v2 on v1

--- a/solution.py
+++ b/solution.py
@@ -101,11 +101,14 @@
     return jnp.concatenate([chunk[0] for chunk in chunks], axis=0)
 
 
-def pre_kernel(n_chunks, groups, k, block, *refs):
-    chunks = refs[:n_chunks]
-    weight, ids, vals = refs[n_chunks:]
+def pre_kernel(n_chunks, groups, k, block, first, *refs):
+    refs = list(refs)
+    chunks = [refs.pop(0) for _ in range(n_chunks)]
+    weight, ids = refs.pop(0), refs.pop(0)
+    before = None if first else refs.pop(0)
+    (vals,) = refs
     rows = stacked(chunks)
-    acc = [jnp.zeros((SUB, LANES), F32)] * (ids.shape[0] // SUB)
+    acc = [jnp.zeros((SUB, LANES), F32)] * (ids.shape[0] // SUB) if first else row_blocks(before)
     for j in range(0, weight.shape[2], block):
         dense = jnp.dot(rows, weight[0, :, j : j + block], preferred_element_type=F32)
         acc = pick(dense, ids, acc, groups, j // LANES, k)
@@ -295,18 +298,23 @@
             parts.append(lax.ppermute(value, "layer", pairs))
         return parts
 
-    args = (*a, enc_weight, tgt)
-    vals = call(
-        functools.partial(pre_kernel, feat, tuple(range(per)), k, block),
-        args, [VMEM] * len(args), VMEM, shape((quarter, LANES), BF16),
-        [], 2 * half_flops, 2 * half_bytes,
-    )
+    vals = []
+    for n, groups in enumerate(halves):
+        first, last = n == 0, n == len(halves) - 1
+        args = (*a[n * per_half : (n + 1) * per_half], enc_weight, tgt, *vals)
+        vals = [
+            call(
+                functools.partial(pre_kernel, per_half, groups, k, block, first),
+                args, [VMEM] * len(args), VMEM, shape((quarter, LANES), BF16 if last else F32),
+                [], half_flops, half_bytes,
+            )
+        ]
     squares, turned = call(
         functools.partial(turn_kernel, feat), a, [VMEM] * feat, [VMEM, VMEM],
         [shape((SUB, LANES), F32), shape((width, tokens), BF16)],
         [], 2 * tokens * width, 4 * half_bytes,
     )
-    pre_parts = exchange(vals)
+    pre_parts = exchange(vals[0])
 
     vals = []
     for n, groups in enumerate(halves):

time: 58.1 us -> 58.1 us (level)
    pallas_call x9 -> x10, Pallas kernels: 18.9 us -> 19.3 us  [call(): pl.pallas_call(kernel, in_specs=in_specs, out_specs=out_specs, out_shape=...]
  transfers between devices with their start and end apart: 20 -> 20, of which waited for: 5 -> 4; matrix products, arithmetic and copies ran while one was open for 0% -> 0% of each run, Pallas kernels for 26% -> 27%
where the time goes in v2:
time: 58.1 us; the launch traced here: 57.9 us
  starting transfers between devices  29.9 us (51%)
  Pallas kernels  19.3 us (33%)
  waiting for transfers between devices  6.97 us (12%)
  local copies, waits for them, and re-layouts  0.91 us (2%)
  between operations  0.83 us (1%)
    ppermute x14, starting transfers between devices, send(): return lax.ppermute(x, 'feat', pairs)  26 us
    pallas_call x10, Pallas kernels, call(): pl.pallas_call(kernel, in_specs=in_specs, out_specs=out_specs, out_shape=...  19.3 us
    ppermute x14, waiting for transfers between devices, send(): return lax.ppermute(x, 'feat', pairs)  6.95 us
    ppermute x6, starting transfers between devices, exchange(): parts.append(lax.ppermute(value, 'layer', pairs))  3.92 us
  transfers between devices with their start and end apart: 20, of which 4 were waited for; matrix products, arithmetic and copies ran while one was open for 0% of the time, Pallas kernels for 27%

profile of v2, /device:TPU:0, one launch (start us, length us, event | category | flops | bytes accessed | tf_op | source)
XLA Modules:
  0.0 57.9 jit_solution(10585336238860456620)
XLA Ops:
  0.6 3.1 %collective-permute-start.7 = (bf16[1,48,2048]{2,1,0:T(8,128)(2,1)}, bf16[1,48,2048]{2,1,0:T(8,128)(2,1)S(1)}, u32[]{:S(2)}, u32[]{:S(2)}) collective-permute-start(bf16[1,48,2048]{2,1,0:T(8,128)(2,1)} %refs_0_.5), channel_id=1, source_target_pairs={{0,2},{1,3},{2,4},{3,5},{4,6},{5,7},{6,0},{7,1},{8,10},{9,11},{10,... | collective-permute-start | bytes 589832 | tf_op jit(solution)/shard_map/ppermute | solution.py:241
  3.7 1.5 %collective-permute-start.12 = (bf16[1,48,2048]{2,1,0:T(8,128)(2,1)}, bf16[1,48,2048]{2,1,0:T(8,128)(2,1)S(1)}, u32[]{:S(2)}, u32[]{:S(2)}) collective-permute-start(bf16[1,48,2048]{2,1,0:T(8,128)(2,1)} %refs_0_.5), channel_id=1, source_target_pairs={{0,1},{1,0},{2,3},{3,2},{4,5},{5,4},{6,7},{7,6},{8,9},{9,8},{10,11... | collective-permute-start | bytes 589832 | tf_op jit(solution)/shard_map/ppermute | solution.py:241
  5.2 2.2 %collective-permute-start.10 = (bf16[1,48,2048]{2,1,0:T(8,128)(2,1)}, bf16[1,48,2048]{2,1,0:T(8,128)(2,1)S(1)}, u32[]{:S(2)}, u32[]{:S(2)}) collective-permute-start(bf16[1,48,2048]{2,1,0:T(8,128)(2,1)} %refs_0_.5), channel_id=1, source_target_pairs={{0,6},{1,7},{2,0},{3,1},{4,2},{5,3},{6,4},{7,5},{8,14},{9,15},{10,... | collective-permute-start | bytes 589832 | tf_op jit(solution)/shard_map/ppermute | solution.py:241
  7.5 1.8 %collective-permute-start.5 = (bf16[1,48,2048]{2,1,0:T(8,128)(2,1)}, bf16[1,48,2048]{2,1,0:T(8,128)(2,1)S(1)}, u32[]{:S(2)}, u32[]{:S(2)}) collective-permute-start(bf16[1,48,2048]{2,1,0:T(8,128)(2,1)} %refs_0_.7), channel_id=1, source_target_pairs={{0,6},{1,7},{2,0},{3,1},{4,2},{5,3},{6,4},{7,5},{8,14},{9,15},{10,... | collective-permute-start | bytes 589832 | tf_op jit(solution)/shard_map/ppermute | solution.py:241
  9.3 0.2 collective-permute-start.1
  9.6 0.8 %copy-done.4 = s32[384,32]{0,1:T(8,128)S(1)} copy-done((s32[384,32]{0,1:T(8,128)S(1)}, s32[384,32]{0,1:T(8,128)}, u32[]{:S(2)}) %copy-start.4) | copy-done | bytes 49176
  10.4 0.8 %shard_map.68.refs_5_.tgt = s32[96,128]{1,0:T(8,128)S(1)} custom-call(s32[9]{0:T(128)S(1)} %stack.39.starts, s32[32,384]{1,0:T(8,128)S(1)} %bitcast.10), custom_call_target="tpu_custom_call" | custom-call | flops 12288 | bytes 196608 | tf_op jit(solution)/shard_map/pallas_call | solution.py:211
  11.2 0.5 collective-permute-done.7.refs_2_
  11.7 6.8 %collective-permute-start.8 = (bf16[1,48,2048]{2,1,0:T(8,128)(2,1)S(1)}, bf16[1,48,2048]{2,1,0:T(8,128)(2,1)S(1)}, u32[]{:S(2)}, u32[]{:S(2)}) collective-permute-start(bf16[1,48,2048]{2,1,0:T(8,128)(2,1)S(1)} %collective-permute-done.7.refs_2_), channel_id=1, source_target_pairs={{0,2},{1,3},{2,4},{3,5},{4,6},{5,7},{6,0},{7,1},{8,10},{9,11},{10,... | collective-permute-start | bytes 589832 | tf_op jit(solution)/shard_map/ppermute | solution.py:241
  18.6 2.5 %shard_map.72.refs_13_.refs_6_ = s32[192,1024]{1,0:T(8,128)S(1)} custom-call(s32[96,128]{1,0:T(8,128)S(1)} %shard_map.68.refs_5_.tgt), custom_call_target="tpu_custom_call" | custom-call | flops 6442450944 | bytes 786432 | tf_op jit(solution)/shard_map/pallas_call | solution.py:211
  21.1 1.9 %collective-permute-start = (bf16[1,48,2048]{2,1,0:T(8,128)(2,1)S(1)}, bf16[1,48,2048]{2,1,0:T(8,128)(2,1)S(1)}, u32[]{:S(2)}, u32[]{:S(2)}) collective-permute-start(bf16[1,48,2048]{2,1,0:T(8,128)(2,1)S(1)} %copy-done.3), channel_id=1, source_target_pairs={{0,1},{1,0},{2,3},{3,2},{4,5},{5,4},{6,7},{7,6},{8,9},{9,8},{10,11... | collective-permute-start | bytes 589832 | tf_op jit(solution)/shard_map/ppermute | solution.py:241
  23.0 0.2 collective-permute-start.13
  23.2 1.8 %collective-permute-start.11 = (bf16[1,48,2048]{2,1,0:T(8,128)(2,1)S(1)}, bf16[1,48,2048]{2,1,0:T(8,128)(2,1)S(1)}, u32[]{:S(2)}, u32[]{:S(2)}) collective-permute-start(bf16[1,48,2048]{2,1,0:T(8,128)(2,1)S(1)} %collective-permute-done.10.refs_2_.refs_6_), channel_id=1, source_target_pairs={{0,1},{1,0},{2,3},{3,2},{4,5},{5,4},{6,7},{7,6},{8,9},{9,8},{10,11... | collective-permute-start | bytes 589832 | tf_op jit(solution)/shard_map/ppermute | solution.py:241
  25.0 1.1 %collective-permute-start.2 = (bf16[1,48,2048]{2,1,0:T(8,128)(2,1)S(1)}, bf16[1,48,2048]{2,1,0:T(8,128)(2,1)S(1)}, u32[]{:S(2)}, u32[]{:S(2)}) collective-permute-start(bf16[1,48,2048]{2,1,0:T(8,128)(2,1)S(1)} %collective-permute-done.1.refs_2_), channel_id=1, source_target_pairs={{0,1},{1,0},{2,3},{3,2},{4,5},{5,4},{6,7},{7,6},{8,9},{9,8},{10,11... | collective-permute-start | bytes 589832 | tf_op jit(solution)/shard_map/ppermute | solution.py:241
  26.1 1.6 %collective-permute-done.8.refs_0_.refs_4_ = bf16[1,48,2048]{2,1,0:T(8,128)(2,1)S(1)} collective-permute-done((bf16[1,48,2048]{2,1,0:T(8,128)(2,1)S(1)}, bf16[1,48,2048]{2,1,0:T(8,128)(2,1)S(1)}, u32[]{:S(2)}, u32[]{:S(2)}) %collective-permute-start.8) | collective-permute-done | bytes 196640 | tf_op jit(solution)/shard_map/ppermute | solution.py:241
  27.7 1.5 %collective-permute-start.9 = (bf16[1,48,2048]{2,1,0:T(8,128)(2,1)S(1)}, bf16[1,48,2048]{2,1,0:T(8,128)(2,1)S(1)}, u32[]{:S(2)}, u32[]{:S(2)}) collective-permute-start(bf16[1,48,2048]{2,1,0:T(8,128)(2,1)S(1)} %collective-permute-done.8.refs_0_.refs_4_), channel_id=1, source_target_pairs={{0,1},{1,0},{2,3},{3,2},{4,5},{5,4},{6,7},{7,6},{8,9},{9,8},{10,11... | collective-permute-start | bytes 589832 | tf_op jit(solution)/shard_map/ppermute | solution.py:241
  29.3 2.5 %shard_map.71.refs_12_.refs_5_ = s32[192,1024]{1,0:T(8,128)S(1)} custom-call(s32[96,128]{1,0:T(8,128)S(1)} %shard_map.68.refs_5_.tgt), custom_call_target="tpu_custom_call" | custom-call | flops 6442450944 | bytes 786432 | tf_op jit(solution)/shard_map/pallas_call | solution.py:211
  31.8 0.7 %collective-permute-start.3 = (bf16[1,48,2048]{2,1,0:T(8,128)(2,1)S(1)}, bf16[1,48,2048]{2,1,0:T(8,128)(2,1)S(1)}, u32[]{:S(2)}, u32[]{:S(2)}) collective-permute-start(bf16[1,48,2048]{2,1,0:T(8,128)(2,1)S(1)} %collective-permute-done.1.refs_2_), channel_id=1, source_target_pairs={{0,2},{1,3},{2,4},{3,5},{4,6},{5,7},{6,0},{7,1},{8,10},{9,11},{10,... | collective-permute-start | bytes 589832 | tf_op jit(solution)/shard_map/ppermute | solution.py:241
  32.5 2.3 %collective-permute-start.6 = (bf16[1,48,2048]{2,1,0:T(8,128)(2,1)S(1)}, bf16[1,48,2048]{2,1,0:T(8,128)(2,1)S(1)}, u32[]{:S(2)}, u32[]{:S(2)}) collective-permute-start(bf16[1,48,2048]{2,1,0:T(8,128)(2,1)S(1)} %collective-permute-done.5.refs_6_.refs_2_), channel_id=1, source_target_pairs={{0,1},{1,0},{2,3},{3,2},{4,5},{5,4},{6,7},{7,6},{8,9},{9,8},{10,11... | collective-permute-start | bytes 589832 | tf_op jit(solution)/shard_map/ppermute | solution.py:241
  34.9 4.6 %collective-permute-done.2.refs_3_ = bf16[1,48,2048]{2,1,0:T(8,128)(2,1)S(1)} collective-permute-done((bf16[1,48,2048]{2,1,0:T(8,128)(2,1)S(1)}, bf16[1,48,2048]{2,1,0:T(8,128)(2,1)S(1)}, u32[]{:S(2)}, u32[]{:S(2)}) %collective-permute-start.2) | collective-permute-done | bytes 196640 | tf_op jit(solution)/shard_map/ppermute | solution.py:241
  39.5 0.8 %collective-permute-start.4 = (bf16[1,48,2048]{2,1,0:T(8,128)(2,1)S(1)}, bf16[1,48,2048]{2,1,0:T(8,128)(2,1)S(1)}, u32[]{:S(2)}, u32[]{:S(2)}) collective-permute-start(bf16[1,48,2048]{2,1,0:T(8,128)(2,1)S(1)} %collective-permute-done.2.refs_3_), channel_id=1, source_target_pairs={{0,2},{1,3},{2,4},{3,5},{4,6},{5,7},{6,0},{7,1},{8,10},{9,11},{10,... | collective-permute-start | bytes 589832 | tf_op jit(solution)/shard_map/ppermute | solution.py:241
  40.2 1.7 %shard_map.75.refs_6_ = f32[96,128]{1,0:T(8,128)S(1)} custom-call(bf16[1,48,2048]{2,1,0:T(8,128)(2,1)S(1)} %copy-done.3, bf16[1,48,2048]{2,1,0:T(8,128)(2,1)S(1)} %collective-permute-done.refs_1_, bf16[1,48,2048]{2,1,0:T(8,128)(2,1)S(1)} %collective-permute-done.1.refs_2_, bf16[1,48,2048]{2,1,0:T(8,128)(2,1)S(1)} %collective-permute-done.2.refs_3_, ...), custom_call_target="tpu_custom_call" | custom-call | flops 805306368 | bytes 786432 | tf_op jit(solution)/shard_map/pallas_call | solution.py:211
  42.0 1.2 %shard_map.69.refs_6_ = f32[96,128]{1,0:T(8,128)S(1)} custom-call(bf16[1,48,2048]{2,1,0:T(8,128)(2,1)S(1)} %copy-done.2, bf16[1,48,2048]{2,1,0:T(8,128)(2,1)S(1)} %collective-permute-done.12.refs_1_, bf16[1,48,2048]{2,1,0:T(8,128)(2,1)S(1)} %collective-permute-done.7.refs_2_, bf16[1,48,2048]{2,1,0:T(8,128)(2,1)S(1)} %collective-permute-done.13.refs_3_, ...), custom_call_target="tpu_custom_call" | custom-call | flops 805306368 | bytes 786432 | tf_op jit(solution)/shard_map/pallas_call | solution.py:211
  43.2 1.2 %shard_map.70.refs_8_ = bf16[96,128]{1,0:T(8,128)(2,1)S(1)} custom-call(bf16[1,48,2048]{2,1,0:T(8,128)(2,1)S(1)} %collective-permute-done.8.refs_0_.refs_4_, bf16[1,48,2048]{2,1,0:T(8,128)(2,1)S(1)} %collective-permute-done.9.refs_1_.refs_5_, bf16[1,48,2048]{2,1,0:T(8,128)(2,1)S(1)} %collective-permute-done.10.refs_2_.refs_6_, ...), custom_call_target="tpu_custom_call" | custom-call | flops 805306368 | bytes 786432 | tf_op jit(solution)/shard_map/pallas_call | solution.py:211
  44.5 1.6 %collective-permute-start.15 = (bf16[96,128]{1,0:T(8,128)(2,1)S(1)}, bf16[96,128]{1,0:T(8,128)(2,1)S(1)}, u32[]{:S(2)}, u32[]{:S(2)}) collective-permute-start(bf16[96,128]{1,0:T(8,128)(2,1)S(1)} %shard_map.70.refs_8_), channel_id=1, source_target_pairs={{0,16},{8,24},{16,0},{24,8},{1,17},{9,25},{17,1},{25,9},{2,18},{10... | collective-permute-start | bytes 73736 | tf_op jit(solution)/shard_map/ppermute | solution.py:298
  46.1 0.5 shard_map.73
  46.6 0.3 collective-permute-start.14
  47.0 1.7 %shard_map.76.refs_0_ = bf16[96,128]{1,0:T(8,128)(2,1)S(1)} custom-call(bf16[1,48,2048]{2,1,0:T(8,128)(2,1)S(1)} %collective-permute-done.3.refs_4_.refs_0_, bf16[1,48,2048]{2,1,0:T(8,128)(2,1)S(1)} %collective-permute-done.4.refs_5_.refs_1_, bf16[1,48,2048]{2,1,0:T(8,128)(2,1)S(1)} %collective-permute-done.5.refs_6_.refs_2_, ...), custom_call_target="tpu_custom_call" | custom-call | flops 805306368 | bytes 786432 | tf_op jit(solution)/shard_map/pallas_call | solution.py:211
  48.7 1.2 %collective-permute-start.19 = (bf16[96,128]{1,0:T(8,128)(2,1)S(1)}, bf16[96,128]{1,0:T(8,128)(2,1)S(1)}, u32[]{:S(2)}, u32[]{:S(2)}) collective-permute-start(bf16[96,128]{1,0:T(8,128)(2,1)S(1)} %shard_map.76.refs_0_), channel_id=1, source_target_pairs={{0,24},{8,16},{16,8},{24,0},{1,25},{9,17},{17,9},{25,1},{2,26},{10... | collective-permute-start | bytes 73736 | tf_op jit(solution)/shard_map/ppermute | solution.py:298
  49.9 0.7 %collective-permute-start.18 = (bf16[96,128]{1,0:T(8,128)(2,1)S(1)}, bf16[96,128]{1,0:T(8,128)(2,1)S(1)}, u32[]{:S(2)}, u32[]{:S(2)}) collective-permute-start(bf16[96,128]{1,0:T(8,128)(2,1)S(1)} %shard_map.76.refs_0_), channel_id=1, source_target_pairs={{0,16},{8,24},{16,0},{24,8},{1,17},{9,25},{17,1},{25,9},{2,18},{10... | collective-permute-start | bytes 73736 | tf_op jit(solution)/shard_map/ppermute | solution.py:298
  50.6 3.6 %shard_map.74 = bf16[1,1024,2048]{2,1,0:T(8,128)(2,1)} custom-call(bf16[1,48,2048]{2,1,0:T(8,128)(2,1)S(1)} %copy-done.3, bf16[1,48,2048]{2,1,0:T(8,128)(2,1)S(1)} %collective-permute-done.refs_1_, bf16[1,48,2048]{2,1,0:T(8,128)(2,1)S(1)} %collective-permute-done.1.refs_2_, bf16[1,48,2048]{2,1,0:T(8,128)(2,1)S(1)} %collective-permute-done.2.refs_3_, ...), custom_call_target="tpu_custom_call" | custom-call | flops 1610612736 | bytes 4194304 | tf_op jit(solution)/shard_map/pallas_call | solution.py:211
  54.3 3.6 %shard_map.77 = bf16[1,2048,1024]{2,1,0:T(8,128)(2,1)} custom-call(bf16[96,128]{1,0:T(8,128)(2,1)S(1)} %shard_map.76.refs_0_, bf16[96,128]{1,0:T(8,128)(2,1)S(1)} %collective-permute-done.17.refs_1_, bf16[96,128]{1,0:T(8,128)(2,1)S(1)} %collective-permute-done.18.refs_2_, bf16[96,128]{1,0:T(8,128)(2,1)S(1)} %collective-permute-done.19.refs_3_, ...), custom_call_target="tpu_custom_call" | custom-call | flops 1610612736 | bytes 4194304 | tf_op jit(solution)/shard_map/pallas_call | solution.py:211
  (29 shorter events, 0.4 us)
Async XLA Ops:
  0.6 11.1 %collective-permute-start.7 = (bf16[1,48,2048]{2,1,0:T(8,128)(2,1)}, bf16[1,48,2048]{2,1,0:T(8,128)(2,1)S(1)}, u32[]{:S(2)}, u32[]{:S(2)}) collective-permute-start(bf16[1,48,2048]{2,1,0:T(8,128)(2,1)} %refs_0_.5), channel_id=1, source_target_pairs={{0,2},{1,3},{2,4},{3,5},{4,6},{5,7},{6,0},{7,1},{8,10},{9,11},{10,... | collective-permute-start | bytes 589832 | tf_op jit(solution)/shard_map/ppermute | solution.py:241
  3.7 17.4 %collective-permute-start.12 = (bf16[1,48,2048]{2,1,0:T(8,128)(2,1)}, bf16[1,48,2048]{2,1,0:T(8,128)(2,1)S(1)}, u32[]{:S(2)}, u32[]{:S(2)}) collective-permute-start(bf16[1,48,2048]{2,1,0:T(8,128)(2,1)} %refs_0_.5), channel_id=1, source_target_pairs={{0,1},{1,0},{2,3},{3,2},{4,5},{5,4},{6,7},{7,6},{8,9},{9,8},{10,11... | collective-permute-start | bytes 589832 | tf_op jit(solution)/shard_map/ppermute | solution.py:241
  5.2 17.8 %collective-permute-start.10 = (bf16[1,48,2048]{2,1,0:T(8,128)(2,1)}, bf16[1,48,2048]{2,1,0:T(8,128)(2,1)S(1)}, u32[]{:S(2)}, u32[]{:S(2)}) collective-permute-start(bf16[1,48,2048]{2,1,0:T(8,128)(2,1)} %refs_0_.5), channel_id=1, source_target_pairs={{0,6},{1,7},{2,0},{3,1},{4,2},{5,3},{6,4},{7,5},{8,14},{9,15},{10,... | collective-permute-start | bytes 589832 | tf_op jit(solution)/shard_map/ppermute | solution.py:241
  7.5 15.7 %collective-permute-start.5 = (bf16[1,48,2048]{2,1,0:T(8,128)(2,1)}, bf16[1,48,2048]{2,1,0:T(8,128)(2,1)S(1)}, u32[]{:S(2)}, u32[]{:S(2)}) collective-permute-start(bf16[1,48,2048]{2,1,0:T(8,128)(2,1)} %refs_0_.7), channel_id=1, source_target_pairs={{0,6},{1,7},{2,0},{3,1},{4,2},{5,3},{6,4},{7,5},{8,14},{9,15},{10,... | collective-permute-start | bytes 589832 | tf_op jit(solution)/shard_map/ppermute | solution.py:241
  9.3 15.8 %collective-permute-start.1 = (bf16[1,48,2048]{2,1,0:T(8,128)(2,1)}, bf16[1,48,2048]{2,1,0:T(8,128)(2,1)S(1)}, u32[]{:S(2)}, u32[]{:S(2)}) collective-permute-start(bf16[1,48,2048]{2,1,0:T(8,128)(2,1)} %refs_0_.7), channel_id=1, source_target_pairs={{0,2},{1,3},{2,4},{3,5},{4,6},{5,7},{6,0},{7,1},{8,10},{9,11},{10,... | collective-permute-start | bytes 589832 | tf_op jit(solution)/shard_map/ppermute | solution.py:241
  9.6 0.8 %copy-start.4 = (s32[384,32]{0,1:T(8,128)S(1)}, s32[384,32]{0,1:T(8,128)}, u32[]{:S(2)}) copy-start(s32[384,32]{0,1:T(8,128)} %param.9) | copy-start | bytes 147460
  11.2 9.9 %copy-start.3 = (bf16[1,48,2048]{2,1,0:T(8,128)(2,1)S(1)}, bf16[1,48,2048]{2,1,0:T(8,128)(2,1)}, u32[]{:S(2)}) copy-start(bf16[1,48,2048]{2,1,0:T(8,128)(2,1)} %refs_0_.7) | copy-start | bytes 589828
  11.7 16.0 %collective-permute-start.8 = (bf16[1,48,2048]{2,1,0:T(8,128)(2,1)S(1)}, bf16[1,48,2048]{2,1,0:T(8,128)(2,1)S(1)}, u32[]{:S(2)}, u32[]{:S(2)}) collective-permute-start(bf16[1,48,2048]{2,1,0:T(8,128)(2,1)S(1)} %collective-permute-done.7.refs_2_), channel_id=1, source_target_pairs={{0,2},{1,3},{2,4},{3,5},{4,6},{5,7},{6,0},{7,1},{8,10},{9,11},{10,... | collective-permute-start | bytes 589832 | tf_op jit(solution)/shard_map/ppermute | solution.py:241
  21.1 19.2 %copy-start.1 = (bf16[1,1024,2048]{2,1,0:T(8,128)(2,1)S(1)}, bf16[1,1024,2048]{2,1,0:T(8,128)(2,1)}, u32[]{:S(2)}) copy-start(bf16[1,1024,2048]{2,1,0:T(8,128)(2,1)} %refs_4_.7) | copy-start | bytes 12582916
  21.1 10.7 %collective-permute-start = (bf16[1,48,2048]{2,1,0:T(8,128)(2,1)S(1)}, bf16[1,48,2048]{2,1,0:T(8,128)(2,1)S(1)}, u32[]{:S(2)}, u32[]{:S(2)}) collective-permute-start(bf16[1,48,2048]{2,1,0:T(8,128)(2,1)S(1)} %copy-done.3), channel_id=1, source_target_pairs={{0,1},{1,0},{2,3},{3,2},{4,5},{5,4},{6,7},{7,6},{8,9},{9,8},{10,11... | collective-permute-start | bytes 589832 | tf_op jit(solution)/shard_map/ppermute | solution.py:241
  23.0 9.5 %collective-permute-start.13 = (bf16[1,48,2048]{2,1,0:T(8,128)(2,1)S(1)}, bf16[1,48,2048]{2,1,0:T(8,128)(2,1)S(1)}, u32[]{:S(2)}, u32[]{:S(2)}) collective-permute-start(bf16[1,48,2048]{2,1,0:T(8,128)(2,1)S(1)} %collective-permute-done.7.refs_2_), channel_id=1, source_target_pairs={{0,1},{1,0},{2,3},{3,2},{4,5},{5,4},{6,7},{7,6},{8,9},{9,8},{10,11... | collective-permute-start | bytes 589832 | tf_op jit(solution)/shard_map/ppermute | solution.py:241
  23.2 20.0 %collective-permute-start.11 = (bf16[1,48,2048]{2,1,0:T(8,128)(2,1)S(1)}, bf16[1,48,2048]{2,1,0:T(8,128)(2,1)S(1)}, u32[]{:S(2)}, u32[]{:S(2)}) collective-permute-start(bf16[1,48,2048]{2,1,0:T(8,128)(2,1)S(1)} %collective-permute-done.10.refs_2_.refs_6_), channel_id=1, source_target_pairs={{0,1},{1,0},{2,3},{3,2},{4,5},{5,4},{6,7},{7,6},{8,9},{9,8},{10,11... | collective-permute-start | bytes 589832 | tf_op jit(solution)/shard_map/ppermute | solution.py:241
  25.0 14.4 %collective-permute-start.2 = (bf16[1,48,2048]{2,1,0:T(8,128)(2,1)S(1)}, bf16[1,48,2048]{2,1,0:T(8,128)(2,1)S(1)}, u32[]{:S(2)}, u32[]{:S(2)}) collective-permute-start(bf16[1,48,2048]{2,1,0:T(8,128)(2,1)S(1)} %collective-permute-done.1.refs_2_), channel_id=1, source_target_pairs={{0,1},{1,0},{2,3},{3,2},{4,5},{5,4},{6,7},{7,6},{8,9},{9,8},{10,11... | collective-permute-start | bytes 589832 | tf_op jit(solution)/shard_map/ppermute | solution.py:241
  27.7 15.5 %collective-permute-start.9 = (bf16[1,48,2048]{2,1,0:T(8,128)(2,1)S(1)}, bf16[1,48,2048]{2,1,0:T(8,128)(2,1)S(1)}, u32[]{:S(2)}, u32[]{:S(2)}) collective-permute-start(bf16[1,48,2048]{2,1,0:T(8,128)(2,1)S(1)} %collective-permute-done.8.refs_0_.refs_4_), channel_id=1, source_target_pairs={{0,1},{1,0},{2,3},{3,2},{4,5},{5,4},{6,7},{7,6},{8,9},{9,8},{10,11... | collective-permute-start | bytes 589832 | tf_op jit(solution)/shard_map/ppermute | solution.py:241
  31.8 10.2 %copy-start = (bf16[1,2048,1024]{2,1,0:T(8,128)(2,1)S(1)}, bf16[1,2048,1024]{2,1,0:T(8,128)(2,1)}, u32[]{:S(2)}) copy-start(bf16[1,2048,1024]{2,1,0:T(8,128)(2,1)} %refs_4_.5) | copy-start | bytes 12582916
  31.8 10.2 %copy-start.2 = (bf16[1,48,2048]{2,1,0:T(8,128)(2,1)S(1)}, bf16[1,48,2048]{2,1,0:T(8,128)(2,1)}, u32[]{:S(2)}) copy-start(bf16[1,48,2048]{2,1,0:T(8,128)(2,1)} %refs_0_.5) | copy-start | bytes 589828
  31.8 15.1 %collective-permute-start.3 = (bf16[1,48,2048]{2,1,0:T(8,128)(2,1)S(1)}, bf16[1,48,2048]{2,1,0:T(8,128)(2,1)S(1)}, u32[]{:S(2)}, u32[]{:S(2)}) collective-permute-start(bf16[1,48,2048]{2,1,0:T(8,128)(2,1)S(1)} %collective-permute-done.1.refs_2_), channel_id=1, source_target_pairs={{0,2},{1,3},{2,4},{3,5},{4,6},{5,7},{6,0},{7,1},{8,10},{9,11},{10,... | collective-permute-start | bytes 589832 | tf_op jit(solution)/shard_map/ppermute | solution.py:241
  32.5 14.0 %collective-permute-start.6 = (bf16[1,48,2048]{2,1,0:T(8,128)(2,1)S(1)}, bf16[1,48,2048]{2,1,0:T(8,128)(2,1)S(1)}, u32[]{:S(2)}, u32[]{:S(2)}) collective-permute-start(bf16[1,48,2048]{2,1,0:T(8,128)(2,1)S(1)} %collective-permute-done.5.refs_6_.refs_2_), channel_id=1, source_target_pairs={{0,1},{1,0},{2,3},{3,2},{4,5},{5,4},{6,7},{7,6},{8,9},{9,8},{10,11... | collective-permute-start | bytes 589832 | tf_op jit(solution)/shard_map/ppermute | solution.py:241
  39.5 7.5 %collective-permute-start.4 = (bf16[1,48,2048]{2,1,0:T(8,128)(2,1)S(1)}, bf16[1,48,2048]{2,1,0:T(8,128)(2,1)S(1)}, u32[]{:S(2)}, u32[]{:S(2)}) collective-permute-start(bf16[1,48,2048]{2,1,0:T(8,128)(2,1)S(1)} %collective-permute-done.2.refs_3_), channel_id=1, source_target_pairs={{0,2},{1,3},{2,4},{3,5},{4,6},{5,7},{6,0},{7,1},{8,10},{9,11},{10,... | collective-permute-start | bytes 589832 | tf_op jit(solution)/shard_map/ppermute | solution.py:241
  44.4 6.2 %collective-permute-start.16 = (bf16[96,128]{1,0:T(8,128)(2,1)S(1)}, bf16[96,128]{1,0:T(8,128)(2,1)S(1)}, u32[]{:S(2)}, u32[]{:S(2)}) collective-permute-start(bf16[96,128]{1,0:T(8,128)(2,1)S(1)} %shard_map.70.refs_8_), channel_id=1, source_target_pairs={{0,24},{8,16},{16,8},{24,0},{1,25},{9,17},{17,9},{25,1},{2,26},{10... | collective-permute-start | bytes 73736 | tf_op jit(solution)/shard_map/ppermute | solution.py:298
  44.5 6.2 %collective-permute-start.15 = (bf16[96,128]{1,0:T(8,128)(2,1)S(1)}, bf16[96,128]{1,0:T(8,128)(2,1)S(1)}, u32[]{:S(2)}, u32[]{:S(2)}) collective-permute-start(bf16[96,128]{1,0:T(8,128)(2,1)S(1)} %shard_map.70.refs_8_), channel_id=1, source_target_pairs={{0,16},{8,24},{16,0},{24,8},{1,17},{9,25},{17,1},{25,9},{2,18},{10... | collective-permute-start | bytes 73736 | tf_op jit(solution)/shard_map/ppermute | solution.py:298
  46.6 4.1 %collective-permute-start.14 = (bf16[96,128]{1,0:T(8,128)(2,1)S(1)}, bf16[96,128]{1,0:T(8,128)(2,1)S(1)}, u32[]{:S(2)}, u32[]{:S(2)}) collective-permute-start(bf16[96,128]{1,0:T(8,128)(2,1)S(1)} %shard_map.70.refs_8_), channel_id=1, source_target_pairs={{0,8},{8,0},{16,24},{24,16},{1,9},{9,1},{17,25},{25,17},{2,10},{10... | collective-permute-start | bytes 73736 | tf_op jit(solution)/shard_map/ppermute | solution.py:298
  48.7 5.6 %collective-permute-start.19 = (bf16[96,128]{1,0:T(8,128)(2,1)S(1)}, bf16[96,128]{1,0:T(8,128)(2,1)S(1)}, u32[]{:S(2)}, u32[]{:S(2)}) collective-permute-start(bf16[96,128]{1,0:T(8,128)(2,1)S(1)} %shard_map.76.refs_0_), channel_id=1, source_target_pairs={{0,24},{8,16},{16,8},{24,0},{1,25},{9,17},{17,9},{25,1},{2,26},{10... | collective-permute-start | bytes 73736 | tf_op jit(solution)/shard_map/ppermute | solution.py:298
  49.9 4.4 %collective-permute-start.18 = (bf16[96,128]{1,0:T(8,128)(2,1)S(1)}, bf16[96,128]{1,0:T(8,128)(2,1)S(1)}, u32[]{:S(2)}, u32[]{:S(2)}) collective-permute-start(bf16[96,128]{1,0:T(8,128)(2,1)S(1)} %shard_map.76.refs_0_), channel_id=1, source_target_pairs={{0,16},{8,24},{16,0},{24,8},{1,17},{9,25},{17,1},{25,9},{2,18},{10... | collective-permute-start | bytes 73736 | tf_op jit(solution)/shard_map/ppermute | solution.py:298
  50.6 3.7 %collective-permute-start.17 = (bf16[96,128]{1,0:T(8,128)(2,1)S(1)}, bf16[96,128]{1,0:T(8,128)(2,1)S(1)}, u32[]{:S(2)}, u32[]{:S(2)}) collective-permute-start(bf16[96,128]{1,0:T(8,128)(2,1)S(1)} %shard_map.76.refs_0_), channel_id=1, source_target_pairs={{0,8},{8,0},{16,24},{24,16},{1,9},{9,1},{17,25},{25,17},{2,10},{10... | collective-permute-start | bytes 73736 | tf_op jit(solution)/shard_map/ppermute | solution.py:298

commit v3 on v2

--- a/solution.py
+++ b/solution.py
@@ -117,7 +117,7 @@
 
 def turn_kernel(n_chunks, *refs):
     chunks = refs[:n_chunks]
-    squares, turned = refs[n_chunks:]
+    scale, turned = refs[n_chunks:]
     rows = stacked(chunks)
     turned[...] = rows.T
     tokens, width = rows.shape
@@ -126,19 +126,15 @@
     part = total[:, :LANES]
     for j in range(LANES, width, LANES):
         part = part + total[:, j : j + LANES]
-    squares[...] = part
-
-
-def scale_of(squares, count):
-    return 2.0 / (jnp.sum(squares[...]) / count + 1e-6)
-
-
-def code_grad_kernel(n_chunks, groups, k, block, first, last, count, *refs):
+    scale[...] = jnp.full(scale.shape, 2.0 / (jnp.sum(part) / (tokens * width) + 1e-6), F32)
+
+
+def code_grad_kernel(n_chunks, groups, k, block, first, last, *refs):
     refs = list(refs)
     chunks = [refs.pop(0) for _ in range(n_chunks)]
     weight, ids = refs.pop(0), refs.pop(0)
     before = None if first else refs.pop(0)
-    squares = refs.pop(0) if last else None
+    scale = refs.pop(0) if last else None
     (vals,) = refs
     rows = stacked(chunks)
     quarter = ids.shape[0]
@@ -148,10 +144,9 @@
             rows, weight[0, j : j + block, :], (((1,), (1,)), ((), ())), preferred_element_type=F32
         )
         acc = pick(dense, ids, acc, groups, j // LANES, k)
-    out = jnp.concatenate(acc, axis=0)
     if last:
-        out = out * scale_of(squares, count)
-    vals[...] = out.astype(vals.dtype)
+        acc = [part * scale[...] for part in acc]
+    vals[...] = jnp.concatenate(acc, axis=0).astype(vals.dtype)
 
 
 def total_of(parts):
@@ -165,11 +160,11 @@
     return [value[m : m + SUB] for m in range(0, value.shape[0], SUB)]
 
 
-def dec_grad_kernel(n_chunks, n_parts, block, count, *refs):
+def dec_grad_kernel(n_chunks, n_parts, block, *refs):
     chunks = refs[:n_chunks]
     parts = refs[n_chunks : n_chunks + n_parts]
-    *inv, squares, out, held, sems = refs[n_chunks + n_parts :]
-    vals = split_rows(total_of(parts) * scale_of(squares, count))
+    *inv, scale, out, held, sems = refs[n_chunks + n_parts :]
+    vals = [part * scale[...] for part in split_rows(total_of(parts))]
     rows = stacked(chunks)
     copies = []
     for n, j in enumerate(range(0, inv[0].shape[1], block)):
@@ -187,17 +182,26 @@
     parts = refs[:n_parts]
     turned, *inv, out, held, sems = refs[n_parts:]
     vals = split_rows(total_of(parts))
+    width, feat_dev = held.shape
+
+    def dense(j):
+        return jnp.concatenate([expand(vals, half, j, block) for half in inv], axis=0).astype(BF16)
+
     copies = []
-    for n, j in enumerate(range(0, inv[0].shape[1], block)):
-        pre_grad = jnp.concatenate([expand(vals, half, j, block) for half in inv], axis=0).astype(BF16)
-        for m in range(0, turned.shape[0], tall):
+    pre_grad = dense(0)
+    for j in range(0, feat_dev, block):
+        last = j + block == feat_dev
+        after = None if last else dense(j + block)
+        reach = width // 2 if last else width
+        for m in range(0, width, tall):
             held[m : m + tall, j : j + block] = jnp.dot(
                 turned[m : m + tall, :], pre_grad, preferred_element_type=F32
             ).astype(BF16)
-        copies.append(
-            pltpu.make_async_copy(held.at[:, pl.ds(j, block)], out.at[0, :, pl.ds(j, block)], sems.at[n])
-        )
-        copies[-1].start()
+            if (m + tall) % reach == 0:
+                part = (pl.ds(m + tall - reach, reach), pl.ds(j, block))
+                copies.append(pltpu.make_async_copy(held.at[part], out.at[(0, *part)], sems.at[len(copies)]))
+                copies[-1].start()
+        pre_grad = after
     for copy in copies:
         copy.wait()
 
@@ -309,7 +313,7 @@
                 [], half_flops, half_bytes,
             )
         ]
-    squares, turned = call(
+    scale, turned = call(
         functools.partial(turn_kernel, feat), a, [VMEM] * feat, [VMEM, VMEM],
         [shape((SUB, LANES), F32), shape((width, tokens), BF16)],
         [], 2 * tokens * width, 4 * half_bytes,
@@ -319,11 +323,11 @@
     vals = []
     for n, groups in enumerate(halves):
         first, last = n == 0, n == len(halves) - 1
-        args = (*e[n * per_half : (n + 1) * per_half], dec_weight, tgt, *vals, *([squares] if last else []))
+        args = (*e[n * per_half : (n + 1) * per_half], dec_weight, tgt, *vals, *([scale] if last else []))
         vals = [
             call(
                 functools.partial(
-                    code_grad_kernel, per_half, groups, k, block, first, last, tokens * width
+                    code_grad_kernel, per_half, groups, k, block, first, last
                 ),
                 args, [VMEM] * len(args), VMEM, shape((quarter, LANES), BF16 if last else F32),
                 [], half_flops, half_bytes,
@@ -332,11 +336,11 @@
     grad_parts = exchange(vals[0])
 
     def out_scratch(rows, columns, block):
-        return [pltpu.VMEM((rows, columns), BF16), pltpu.SemaphoreType.DMA((feat_dev // block,))]
-
-    args = (*e, *pre_parts, *inv, squares)
+        return [pltpu.VMEM((rows, columns), BF16), pltpu.SemaphoreType.DMA((feat_dev // block + 1,))]
+
+    args = (*e, *pre_parts, *inv, scale)
     dec_grad = call(
-        functools.partial(dec_grad_kernel, feat, n_layer, LANES, tokens * width),
+        functools.partial(dec_grad_kernel, feat, n_layer, LANES),
         args, [VMEM] * len(args), ANY, shape((1, feat_dev, width), BF16),
         out_scratch(feat_dev, width, LANES), 2 * half_flops, 2 * feat_dev * width,
     )

time: 58.1 us -> 58.1 us (level)
  transfers between devices with their start and end apart: 20 -> 20, of which waited for: 4 -> 3; matrix products, arithmetic and copies ran while one was open for 0% -> 0% of each run, Pallas kernels for 27% -> 27%
where the time goes in v3:
time: 58.1 us; the launch traced here: 57.9 us
  starting transfers between devices  29.9 us (51%)
  Pallas kernels  19.4 us (33%)
  waiting for transfers between devices  6.89 us (12%)
  local copies, waits for them, and re-layouts  0.91 us (2%)
  between operations  0.84 us (1%)
    ppermute x14, starting transfers between devices, send(): return lax.ppermute(x, 'feat', pairs)  26 us
    pallas_call x10, Pallas kernels, call(): pl.pallas_call(kernel, in_specs=in_specs, out_specs=out_specs, out_shape=...  19.4 us
    ppermute x14, waiting for transfers between devices, send(): return lax.ppermute(x, 'feat', pairs)  6.87 us
    ppermute x6, starting transfers between devices, exchange(): parts.append(lax.ppermute(value, 'layer', pairs))  3.97 us
  transfers between devices with their start and end apart: 20, of which 3 were waited for; matrix products, arithmetic and copies ran while one was open for 0% of the time, Pallas kernels for 27%

profile of v3, /device:TPU:0, one launch (start us, length us, event | category | flops | bytes accessed | tf_op | source)
XLA Modules:
  0.0 57.9 jit_solution(8624681741540793086)
XLA Ops:
  0.6 3.1 %collective-permute-start.7 = (bf16[1,48,2048]{2,1,0:T(8,128)(2,1)}, bf16[1,48,2048]{2,1,0:T(8,128)(2,1)S(1)}, u32[]{:S(2)}, u32[]{:S(2)}) collective-permute-start(bf16[1,48,2048]{2,1,0:T(8,128)(2,1)} %refs_0_.5), channel_id=1, source_target_pairs={{0,2},{1,3},{2,4},{3,5},{4,6},{5,7},{6,0},{7,1},{8,10},{9,11},{10,... | collective-permute-start | bytes 589832 | tf_op jit(solution)/shard_map/ppermute | solution.py:245
  3.7 1.5 %collective-permute-start.12 = (bf16[1,48,2048]{2,1,0:T(8,128)(2,1)}, bf16[1,48,2048]{2,1,0:T(8,128)(2,1)S(1)}, u32[]{:S(2)}, u32[]{:S(2)}) collective-permute-start(bf16[1,48,2048]{2,1,0:T(8,128)(2,1)} %refs_0_.5), channel_id=1, source_target_pairs={{0,1},{1,0},{2,3},{3,2},{4,5},{5,4},{6,7},{7,6},{8,9},{9,8},{10,11... | collective-permute-start | bytes 589832 | tf_op jit(solution)/shard_map/ppermute | solution.py:245
  5.2 2.2 %collective-permute-start.10 = (bf16[1,48,2048]{2,1,0:T(8,128)(2,1)}, bf16[1,48,2048]{2,1,0:T(8,128)(2,1)S(1)}, u32[]{:S(2)}, u32[]{:S(2)}) collective-permute-start(bf16[1,48,2048]{2,1,0:T(8,128)(2,1)} %refs_0_.5), channel_id=1, source_target_pairs={{0,6},{1,7},{2,0},{3,1},{4,2},{5,3},{6,4},{7,5},{8,14},{9,15},{10,... | collective-permute-start | bytes 589832 | tf_op jit(solution)/shard_map/ppermute | solution.py:245
  7.5 1.8 %collective-permute-start.5 = (bf16[1,48,2048]{2,1,0:T(8,128)(2,1)}, bf16[1,48,2048]{2,1,0:T(8,128)(2,1)S(1)}, u32[]{:S(2)}, u32[]{:S(2)}) collective-permute-start(bf16[1,48,2048]{2,1,0:T(8,128)(2,1)} %refs_0_.7), channel_id=1, source_target_pairs={{0,6},{1,7},{2,0},{3,1},{4,2},{5,3},{6,4},{7,5},{8,14},{9,15},{10,... | collective-permute-start | bytes 589832 | tf_op jit(solution)/shard_map/ppermute | solution.py:245
  9.3 0.2 collective-permute-start.1
  9.6 0.8 %copy-done.4 = s32[384,32]{0,1:T(8,128)S(1)} copy-done((s32[384,32]{0,1:T(8,128)S(1)}, s32[384,32]{0,1:T(8,128)}, u32[]{:S(2)}) %copy-start.4) | copy-done | bytes 49176
  10.4 0.8 %shard_map.68.refs_5_.tgt = s32[96,128]{1,0:T(8,128)S(1)} custom-call(s32[9]{0:T(128)S(1)} %stack.39.starts, s32[32,384]{1,0:T(8,128)S(1)} %bitcast.10), custom_call_target="tpu_custom_call" | custom-call | flops 12288 | bytes 196608 | tf_op jit(solution)/shard_map/pallas_call | solution.py:215
  11.2 0.5 collective-permute-done.7.refs_2_
  11.7 6.8 %collective-permute-start.8 = (bf16[1,48,2048]{2,1,0:T(8,128)(2,1)S(1)}, bf16[1,48,2048]{2,1,0:T(8,128)(2,1)S(1)}, u32[]{:S(2)}, u32[]{:S(2)}) collective-permute-start(bf16[1,48,2048]{2,1,0:T(8,128)(2,1)S(1)} %collective-permute-done.7.refs_2_), channel_id=1, source_target_pairs={{0,2},{1,3},{2,4},{3,5},{4,6},{5,7},{6,0},{7,1},{8,10},{9,11},{10,... | collective-permute-start | bytes 589832 | tf_op jit(solution)/shard_map/ppermute | solution.py:245
  18.6 2.5 %shard_map.72.refs_13_.refs_6_ = s32[192,1024]{1,0:T(8,128)S(1)} custom-call(s32[96,128]{1,0:T(8,128)S(1)} %shard_map.68.refs_5_.tgt), custom_call_target="tpu_custom_call" | custom-call | flops 6442450944 | bytes 786432 | tf_op jit(solution)/shard_map/pallas_call | solution.py:215
  21.1 1.9 %collective-permute-start = (bf16[1,48,2048]{2,1,0:T(8,128)(2,1)S(1)}, bf16[1,48,2048]{2,1,0:T(8,128)(2,1)S(1)}, u32[]{:S(2)}, u32[]{:S(2)}) collective-permute-start(bf16[1,48,2048]{2,1,0:T(8,128)(2,1)S(1)} %copy-done.3), channel_id=1, source_target_pairs={{0,1},{1,0},{2,3},{3,2},{4,5},{5,4},{6,7},{7,6},{8,9},{9,8},{10,11... | collective-permute-start | bytes 589832 | tf_op jit(solution)/shard_map/ppermute | solution.py:245
  23.0 0.2 collective-permute-start.13
  23.2 1.8 %collective-permute-start.11 = (bf16[1,48,2048]{2,1,0:T(8,128)(2,1)S(1)}, bf16[1,48,2048]{2,1,0:T(8,128)(2,1)S(1)}, u32[]{:S(2)}, u32[]{:S(2)}) collective-permute-start(bf16[1,48,2048]{2,1,0:T(8,128)(2,1)S(1)} %collective-permute-done.10.refs_2_.refs_6_), channel_id=1, source_target_pairs={{0,1},{1,0},{2,3},{3,2},{4,5},{5,4},{6,7},{7,6},{8,9},{9,8},{10,11... | collective-permute-start | bytes 589832 | tf_op jit(solution)/shard_map/ppermute | solution.py:245
  25.0 1.1 %collective-permute-start.2 = (bf16[1,48,2048]{2,1,0:T(8,128)(2,1)S(1)}, bf16[1,48,2048]{2,1,0:T(8,128)(2,1)S(1)}, u32[]{:S(2)}, u32[]{:S(2)}) collective-permute-start(bf16[1,48,2048]{2,1,0:T(8,128)(2,1)S(1)} %collective-permute-done.1.refs_2_), channel_id=1, source_target_pairs={{0,1},{1,0},{2,3},{3,2},{4,5},{5,4},{6,7},{7,6},{8,9},{9,8},{10,11... | collective-permute-start | bytes 589832 | tf_op jit(solution)/shard_map/ppermute | solution.py:245
  26.1 1.6 %collective-permute-done.8.refs_0_.refs_4_ = bf16[1,48,2048]{2,1,0:T(8,128)(2,1)S(1)} collective-permute-done((bf16[1,48,2048]{2,1,0:T(8,128)(2,1)S(1)}, bf16[1,48,2048]{2,1,0:T(8,128)(2,1)S(1)}, u32[]{:S(2)}, u32[]{:S(2)}) %collective-permute-start.8) | collective-permute-done | bytes 196640 | tf_op jit(solution)/shard_map/ppermute | solution.py:245
  27.7 1.5 %collective-permute-start.9 = (bf16[1,48,2048]{2,1,0:T(8,128)(2,1)S(1)}, bf16[1,48,2048]{2,1,0:T(8,128)(2,1)S(1)}, u32[]{:S(2)}, u32[]{:S(2)}) collective-permute-start(bf16[1,48,2048]{2,1,0:T(8,128)(2,1)S(1)} %collective-permute-done.8.refs_0_.refs_4_), channel_id=1, source_target_pairs={{0,1},{1,0},{2,3},{3,2},{4,5},{5,4},{6,7},{7,6},{8,9},{9,8},{10,11... | collective-permute-start | bytes 589832 | tf_op jit(solution)/shard_map/ppermute | solution.py:245
  29.3 2.5 %shard_map.71.refs_12_.refs_5_ = s32[192,1024]{1,0:T(8,128)S(1)} custom-call(s32[96,128]{1,0:T(8,128)S(1)} %shard_map.68.refs_5_.tgt), custom_call_target="tpu_custom_call" | custom-call | flops 6442450944 | bytes 786432 | tf_op jit(solution)/shard_map/pallas_call | solution.py:215
  31.8 0.7 %collective-permute-start.3 = (bf16[1,48,2048]{2,1,0:T(8,128)(2,1)S(1)}, bf16[1,48,2048]{2,1,0:T(8,128)(2,1)S(1)}, u32[]{:S(2)}, u32[]{:S(2)}) collective-permute-start(bf16[1,48,2048]{2,1,0:T(8,128)(2,1)S(1)} %collective-permute-done.1.refs_2_), channel_id=1, source_target_pairs={{0,2},{1,3},{2,4},{3,5},{4,6},{5,7},{6,0},{7,1},{8,10},{9,11},{10,... | collective-permute-start | bytes 589832 | tf_op jit(solution)/shard_map/ppermute | solution.py:245
  32.5 2.3 %collective-permute-start.6 = (bf16[1,48,2048]{2,1,0:T(8,128)(2,1)S(1)}, bf16[1,48,2048]{2,1,0:T(8,128)(2,1)S(1)}, u32[]{:S(2)}, u32[]{:S(2)}) collective-permute-start(bf16[1,48,2048]{2,1,0:T(8,128)(2,1)S(1)} %collective-permute-done.5.refs_6_.refs_2_), channel_id=1, source_target_pairs={{0,1},{1,0},{2,3},{3,2},{4,5},{5,4},{6,7},{7,6},{8,9},{9,8},{10,11... | collective-permute-start | bytes 589832 | tf_op jit(solution)/shard_map/ppermute | solution.py:245
  34.9 4.6 %collective-permute-done.2.refs_3_ = bf16[1,48,2048]{2,1,0:T(8,128)(2,1)S(1)} collective-permute-done((bf16[1,48,2048]{2,1,0:T(8,128)(2,1)S(1)}, bf16[1,48,2048]{2,1,0:T(8,128)(2,1)S(1)}, u32[]{:S(2)}, u32[]{:S(2)}) %collective-permute-start.2) | collective-permute-done | bytes 196640 | tf_op jit(solution)/shard_map/ppermute | solution.py:245
  39.5 0.8 %collective-permute-start.4 = (bf16[1,48,2048]{2,1,0:T(8,128)(2,1)S(1)}, bf16[1,48,2048]{2,1,0:T(8,128)(2,1)S(1)}, u32[]{:S(2)}, u32[]{:S(2)}) collective-permute-start(bf16[1,48,2048]{2,1,0:T(8,128)(2,1)S(1)} %collective-permute-done.2.refs_3_), channel_id=1, source_target_pairs={{0,2},{1,3},{2,4},{3,5},{4,6},{5,7},{6,0},{7,1},{8,10},{9,11},{10,... | collective-permute-start | bytes 589832 | tf_op jit(solution)/shard_map/ppermute | solution.py:245
  40.2 1.7 %shard_map.75.refs_6_ = f32[96,128]{1,0:T(8,128)S(1)} custom-call(bf16[1,48,2048]{2,1,0:T(8,128)(2,1)S(1)} %copy-done.3, bf16[1,48,2048]{2,1,0:T(8,128)(2,1)S(1)} %collective-permute-done.refs_1_, bf16[1,48,2048]{2,1,0:T(8,128)(2,1)S(1)} %collective-permute-done.1.refs_2_, bf16[1,48,2048]{2,1,0:T(8,128)(2,1)S(1)} %collective-permute-done.2.refs_3_, ...), custom_call_target="tpu_custom_call" | custom-call | flops 805306368 | bytes 786432 | tf_op jit(solution)/shard_map/pallas_call | solution.py:215
  42.0 1.2 %shard_map.69.refs_6_ = f32[96,128]{1,0:T(8,128)S(1)} custom-call(bf16[1,48,2048]{2,1,0:T(8,128)(2,1)S(1)} %copy-done.2, bf16[1,48,2048]{2,1,0:T(8,128)(2,1)S(1)} %collective-permute-done.12.refs_1_, bf16[1,48,2048]{2,1,0:T(8,128)(2,1)S(1)} %collective-permute-done.7.refs_2_, bf16[1,48,2048]{2,1,0:T(8,128)(2,1)S(1)} %collective-permute-done.13.refs_3_, ...), custom_call_target="tpu_custom_call" | custom-call | flops 805306368 | bytes 786432 | tf_op jit(solution)/shard_map/pallas_call | solution.py:215
  43.2 1.2 %shard_map.70.refs_8_ = bf16[96,128]{1,0:T(8,128)(2,1)S(1)} custom-call(bf16[1,48,2048]{2,1,0:T(8,128)(2,1)S(1)} %collective-permute-done.8.refs_0_.refs_4_, bf16[1,48,2048]{2,1,0:T(8,128)(2,1)S(1)} %collective-permute-done.9.refs_1_.refs_5_, bf16[1,48,2048]{2,1,0:T(8,128)(2,1)S(1)} %collective-permute-done.10.refs_2_.refs_6_, ...), custom_call_target="tpu_custom_call" | custom-call | flops 805306368 | bytes 786432 | tf_op jit(solution)/shard_map/pallas_call | solution.py:215
  44.5 1.6 %collective-permute-start.15 = (bf16[96,128]{1,0:T(8,128)(2,1)S(1)}, bf16[96,128]{1,0:T(8,128)(2,1)S(1)}, u32[]{:S(2)}, u32[]{:S(2)}) collective-permute-start(bf16[96,128]{1,0:T(8,128)(2,1)S(1)} %shard_map.70.refs_8_), channel_id=1, source_target_pairs={{0,16},{8,24},{16,0},{24,8},{1,17},{9,25},{17,1},{25,9},{2,18},{10... | collective-permute-start | bytes 73736 | tf_op jit(solution)/shard_map/ppermute | solution.py:302
  46.1 0.9 %shard_map.73 = (f32[8,128]{1,0:T(8,128)S(1)}, bf16[2048,384]{1,0:T(8,128)(2,1)S(1)}) custom-call(bf16[1,48,2048]{2,1,0:T(8,128)(2,1)S(1)} %copy-done.2, bf16[1,48,2048]{2,1,0:T(8,128)(2,1)S(1)} %collective-permute-done.12.refs_1_, bf16[1,48,2048]{2,1,0:T(8,128)(2,1)S(1)} %collective-permute-done.7.refs_2_, ...), custom_call_target="tpu_custom_call" | custom-call | flops 1572864 | bytes 3145728 | tf_op jit(solution)/shard_map/pallas_call | solution.py:215
  47.0 0.3 collective-permute-start.14
  47.3 1.7 %shard_map.76.refs_0_ = bf16[96,128]{1,0:T(8,128)(2,1)S(1)} custom-call(bf16[1,48,2048]{2,1,0:T(8,128)(2,1)S(1)} %collective-permute-done.3.refs_4_.refs_0_, bf16[1,48,2048]{2,1,0:T(8,128)(2,1)S(1)} %collective-permute-done.4.refs_5_.refs_1_, bf16[1,48,2048]{2,1,0:T(8,128)(2,1)S(1)} %collective-permute-done.5.refs_6_.refs_2_, ...), custom_call_target="tpu_custom_call" | custom-call | flops 805306368 | bytes 786432 | tf_op jit(solution)/shard_map/pallas_call | solution.py:215
  49.0 1.3 %collective-permute-start.19 = (bf16[96,128]{1,0:T(8,128)(2,1)S(1)}, bf16[96,128]{1,0:T(8,128)(2,1)S(1)}, u32[]{:S(2)}, u32[]{:S(2)}) collective-permute-start(bf16[96,128]{1,0:T(8,128)(2,1)S(1)} %shard_map.76.refs_0_), channel_id=1, source_target_pairs={{0,24},{8,16},{16,8},{24,0},{1,25},{9,17},{17,9},{25,1},{2,26},{10... | collective-permute-start | bytes 73736 | tf_op jit(solution)/shard_map/ppermute | solution.py:302
  50.3 0.7 %collective-permute-start.18 = (bf16[96,128]{1,0:T(8,128)(2,1)S(1)}, bf16[96,128]{1,0:T(8,128)(2,1)S(1)}, u32[]{:S(2)}, u32[]{:S(2)}) collective-permute-start(bf16[96,128]{1,0:T(8,128)(2,1)S(1)} %shard_map.76.refs_0_), channel_id=1, source_target_pairs={{0,16},{8,24},{16,0},{24,8},{1,17},{9,25},{17,1},{25,9},{2,18},{10... | collective-permute-start | bytes 73736 | tf_op jit(solution)/shard_map/ppermute | solution.py:302
  51.0 3.5 %shard_map.74 = bf16[1,1024,2048]{2,1,0:T(8,128)(2,1)} custom-call(bf16[1,48,2048]{2,1,0:T(8,128)(2,1)S(1)} %copy-done.3, bf16[1,48,2048]{2,1,0:T(8,128)(2,1)S(1)} %collective-permute-done.refs_1_, bf16[1,48,2048]{2,1,0:T(8,128)(2,1)S(1)} %collective-permute-done.1.refs_2_, bf16[1,48,2048]{2,1,0:T(8,128)(2,1)S(1)} %collective-permute-done.2.refs_3_, ...), custom_call_target="tpu_custom_call" | custom-call | flops 1610612736 | bytes 4194304 | tf_op jit(solution)/shard_map/pallas_call | solution.py:215
  54.5 3.4 %shard_map.77 = bf16[1,2048,1024]{2,1,0:T(8,128)(2,1)} custom-call(bf16[96,128]{1,0:T(8,128)(2,1)S(1)} %shard_map.76.refs_0_, bf16[96,128]{1,0:T(8,128)(2,1)S(1)} %collective-permute-done.17.refs_1_, bf16[96,128]{1,0:T(8,128)(2,1)S(1)} %collective-permute-done.18.refs_2_, bf16[96,128]{1,0:T(8,128)(2,1)S(1)} %collective-permute-done.19.refs_3_, ...), custom_call_target="tpu_custom_call" | custom-call | flops 1610612736 | bytes 4194304 | tf_op jit(solution)/shard_map/pallas_call | solution.py:215
  (29 shorter events, 0.3 us)
Async XLA Ops:
  0.6 11.1 %collective-permute-start.7 = (bf16[1,48,2048]{2,1,0:T(8,128)(2,1)}, bf16[1,48,2048]{2,1,0:T(8,128)(2,1)S(1)}, u32[]{:S(2)}, u32[]{:S(2)}) collective-permute-start(bf16[1,48,2048]{2,1,0:T(8,128)(2,1)} %refs_0_.5), channel_id=1, source_target_pairs={{0,2},{1,3},{2,4},{3,5},{4,6},{5,7},{6,0},{7,1},{8,10},{9,11},{10,... | collective-permute-start | bytes 589832 | tf_op jit(solution)/shard_map/ppermute | solution.py:245
  3.7 17.4 %collective-permute-start.12 = (bf16[1,48,2048]{2,1,0:T(8,128)(2,1)}, bf16[1,48,2048]{2,1,0:T(8,128)(2,1)S(1)}, u32[]{:S(2)}, u32[]{:S(2)}) collective-permute-start(bf16[1,48,2048]{2,1,0:T(8,128)(2,1)} %refs_0_.5), channel_id=1, source_target_pairs={{0,1},{1,0},{2,3},{3,2},{4,5},{5,4},{6,7},{7,6},{8,9},{9,8},{10,11... | collective-permute-start | bytes 589832 | tf_op jit(solution)/shard_map/ppermute | solution.py:245
  5.2 17.8 %collective-permute-start.10 = (bf16[1,48,2048]{2,1,0:T(8,128)(2,1)}, bf16[1,48,2048]{2,1,0:T(8,128)(2,1)S(1)}, u32[]{:S(2)}, u32[]{:S(2)}) collective-permute-start(bf16[1,48,2048]{2,1,0:T(8,128)(2,1)} %refs_0_.5), channel_id=1, source_target_pairs={{0,6},{1,7},{2,0},{3,1},{4,2},{5,3},{6,4},{7,5},{8,14},{9,15},{10,... | collective-permute-start | bytes 589832 | tf_op jit(solution)/shard_map/ppermute | solution.py:245
  7.5 15.7 %collective-permute-start.5 = (bf16[1,48,2048]{2,1,0:T(8,128)(2,1)}, bf16[1,48,2048]{2,1,0:T(8,128)(2,1)S(1)}, u32[]{:S(2)}, u32[]{:S(2)}) collective-permute-start(bf16[1,48,2048]{2,1,0:T(8,128)(2,1)} %refs_0_.7), channel_id=1, source_target_pairs={{0,6},{1,7},{2,0},{3,1},{4,2},{5,3},{6,4},{7,5},{8,14},{9,15},{10,... | collective-permute-start | bytes 589832 | tf_op jit(solution)/shard_map/ppermute | solution.py:245
  9.3 15.8 %collective-permute-start.1 = (bf16[1,48,2048]{2,1,0:T(8,128)(2,1)}, bf16[1,48,2048]{2,1,0:T(8,128)(2,1)S(1)}, u32[]{:S(2)}, u32[]{:S(2)}) collective-permute-start(bf16[1,48,2048]{2,1,0:T(8,128)(2,1)} %refs_0_.7), channel_id=1, source_target_pairs={{0,2},{1,3},{2,4},{3,5},{4,6},{5,7},{6,0},{7,1},{8,10},{9,11},{10,... | collective-permute-start | bytes 589832 | tf_op jit(solution)/shard_map/ppermute | solution.py:245
  9.6 0.8 %copy-start.4 = (s32[384,32]{0,1:T(8,128)S(1)}, s32[384,32]{0,1:T(8,128)}, u32[]{:S(2)}) copy-start(s32[384,32]{0,1:T(8,128)} %param.9) | copy-start | bytes 147460
  11.2 9.9 %copy-start.3 = (bf16[1,48,2048]{2,1,0:T(8,128)(2,1)S(1)}, bf16[1,48,2048]{2,1,0:T(8,128)(2,1)}, u32[]{:S(2)}) copy-start(bf16[1,48,2048]{2,1,0:T(8,128)(2,1)} %refs_0_.7) | copy-start | bytes 589828
  11.7 16.0 %collective-permute-start.8 = (bf16[1,48,2048]{2,1,0:T(8,128)(2,1)S(1)}, bf16[1,48,2048]{2,1,0:T(8,128)(2,1)S(1)}, u32[]{:S(2)}, u32[]{:S(2)}) collective-permute-start(bf16[1,48,2048]{2,1,0:T(8,128)(2,1)S(1)} %collective-permute-done.7.refs_2_), channel_id=1, source_target_pairs={{0,2},{1,3},{2,4},{3,5},{4,6},{5,7},{6,0},{7,1},{8,10},{9,11},{10,... | collective-permute-start | bytes 589832 | tf_op jit(solution)/shard_map/ppermute | solution.py:245
  21.1 19.2 %copy-start.1 = (bf16[1,1024,2048]{2,1,0:T(8,128)(2,1)S(1)}, bf16[1,1024,2048]{2,1,0:T(8,128)(2,1)}, u32[]{:S(2)}) copy-start(bf16[1,1024,2048]{2,1,0:T(8,128)(2,1)} %refs_4_.7) | copy-start | bytes 12582916
  21.1 10.7 %collective-permute-start = (bf16[1,48,2048]{2,1,0:T(8,128)(2,1)S(1)}, bf16[1,48,2048]{2,1,0:T(8,128)(2,1)S(1)}, u32[]{:S(2)}, u32[]{:S(2)}) collective-permute-start(bf16[1,48,2048]{2,1,0:T(8,128)(2,1)S(1)} %copy-done.3), channel_id=1, source_target_pairs={{0,1},{1,0},{2,3},{3,2},{4,5},{5,4},{6,7},{7,6},{8,9},{9,8},{10,11... | collective-permute-start | bytes 589832 | tf_op jit(solution)/shard_map/ppermute | solution.py:245
  23.0 9.5 %collective-permute-start.13 = (bf16[1,48,2048]{2,1,0:T(8,128)(2,1)S(1)}, bf16[1,48,2048]{2,1,0:T(8,128)(2,1)S(1)}, u32[]{:S(2)}, u32[]{:S(2)}) collective-permute-start(bf16[1,48,2048]{2,1,0:T(8,128)(2,1)S(1)} %collective-permute-done.7.refs_2_), channel_id=1, source_target_pairs={{0,1},{1,0},{2,3},{3,2},{4,5},{5,4},{6,7},{7,6},{8,9},{9,8},{10,11... | collective-permute-start | bytes 589832 | tf_op jit(solution)/shard_map/ppermute | solution.py:245
  23.2 20.0 %collective-permute-start.11 = (bf16[1,48,2048]{2,1,0:T(8,128)(2,1)S(1)}, bf16[1,48,2048]{2,1,0:T(8,128)(2,1)S(1)}, u32[]{:S(2)}, u32[]{:S(2)}) collective-permute-start(bf16[1,48,2048]{2,1,0:T(8,128)(2,1)S(1)} %collective-permute-done.10.refs_2_.refs_6_), channel_id=1, source_target_pairs={{0,1},{1,0},{2,3},{3,2},{4,5},{5,4},{6,7},{7,6},{8,9},{9,8},{10,11... | collective-permute-start | bytes 589832 | tf_op jit(solution)/shard_map/ppermute | solution.py:245
  25.0 14.4 %collective-permute-start.2 = (bf16[1,48,2048]{2,1,0:T(8,128)(2,1)S(1)}, bf16[1,48,2048]{2,1,0:T(8,128)(2,1)S(1)}, u32[]{:S(2)}, u32[]{:S(2)}) collective-permute-start(bf16[1,48,2048]{2,1,0:T(8,128)(2,1)S(1)} %collective-permute-done.1.refs_2_), channel_id=1, source_target_pairs={{0,1},{1,0},{2,3},{3,2},{4,5},{5,4},{6,7},{7,6},{8,9},{9,8},{10,11... | collective-permute-start | bytes 589832 | tf_op jit(solution)/shard_map/ppermute | solution.py:245
  27.7 15.5 %collective-permute-start.9 = (bf16[1,48,2048]{2,1,0:T(8,128)(2,1)S(1)}, bf16[1,48,2048]{2,1,0:T(8,128)(2,1)S(1)}, u32[]{:S(2)}, u32[]{:S(2)}) collective-permute-start(bf16[1,48,2048]{2,1,0:T(8,128)(2,1)S(1)} %collective-permute-done.8.refs_0_.refs_4_), channel_id=1, source_target_pairs={{0,1},{1,0},{2,3},{3,2},{4,5},{5,4},{6,7},{7,6},{8,9},{9,8},{10,11... | collective-permute-start | bytes 589832 | tf_op jit(solution)/shard_map/ppermute | solution.py:245
  31.8 10.2 %copy-start = (bf16[1,2048,1024]{2,1,0:T(8,128)(2,1)S(1)}, bf16[1,2048,1024]{2,1,0:T(8,128)(2,1)}, u32[]{:S(2)}) copy-start(bf16[1,2048,1024]{2,1,0:T(8,128)(2,1)} %refs_4_.5) | copy-start | bytes 12582916
  31.8 10.2 %copy-start.2 = (bf16[1,48,2048]{2,1,0:T(8,128)(2,1)S(1)}, bf16[1,48,2048]{2,1,0:T(8,128)(2,1)}, u32[]{:S(2)}) copy-start(bf16[1,48,2048]{2,1,0:T(8,128)(2,1)} %refs_0_.5) | copy-start | bytes 589828
  31.8 15.5 %collective-permute-start.3 = (bf16[1,48,2048]{2,1,0:T(8,128)(2,1)S(1)}, bf16[1,48,2048]{2,1,0:T(8,128)(2,1)S(1)}, u32[]{:S(2)}, u32[]{:S(2)}) collective-permute-start(bf16[1,48,2048]{2,1,0:T(8,128)(2,1)S(1)} %collective-permute-done.1.refs_2_), channel_id=1, source_target_pairs={{0,2},{1,3},{2,4},{3,5},{4,6},{5,7},{6,0},{7,1},{8,10},{9,11},{10,... | collective-permute-start | bytes 589832 | tf_op jit(solution)/shard_map/ppermute | solution.py:245
  32.5 14.4 %collective-permute-start.6 = (bf16[1,48,2048]{2,1,0:T(8,128)(2,1)S(1)}, bf16[1,48,2048]{2,1,0:T(8,128)(2,1)S(1)}, u32[]{:S(2)}, u32[]{:S(2)}) collective-permute-start(bf16[1,48,2048]{2,1,0:T(8,128)(2,1)S(1)} %collective-permute-done.5.refs_6_.refs_2_), channel_id=1, source_target_pairs={{0,1},{1,0},{2,3},{3,2},{4,5},{5,4},{6,7},{7,6},{8,9},{9,8},{10,11... | collective-permute-start | bytes 589832 | tf_op jit(solution)/shard_map/ppermute | solution.py:245
  39.5 7.8 %collective-permute-start.4 = (bf16[1,48,2048]{2,1,0:T(8,128)(2,1)S(1)}, bf16[1,48,2048]{2,1,0:T(8,128)(2,1)S(1)}, u32[]{:S(2)}, u32[]{:S(2)}) collective-permute-start(bf16[1,48,2048]{2,1,0:T(8,128)(2,1)S(1)} %collective-permute-done.2.refs_3_), channel_id=1, source_target_pairs={{0,2},{1,3},{2,4},{3,5},{4,6},{5,7},{6,0},{7,1},{8,10},{9,11},{10,... | collective-permute-start | bytes 589832 | tf_op jit(solution)/shard_map/ppermute | solution.py:245
  44.4 6.6 %collective-permute-start.16 = (bf16[96,128]{1,0:T(8,128)(2,1)S(1)}, bf16[96,128]{1,0:T(8,128)(2,1)S(1)}, u32[]{:S(2)}, u32[]{:S(2)}) collective-permute-start(bf16[96,128]{1,0:T(8,128)(2,1)S(1)} %shard_map.70.refs_8_), channel_id=1, source_target_pairs={{0,24},{8,16},{16,8},{24,0},{1,25},{9,17},{17,9},{25,1},{2,26},{10... | collective-permute-start | bytes 73736 | tf_op jit(solution)/shard_map/ppermute | solution.py:302
  44.5 6.5 %collective-permute-start.15 = (bf16[96,128]{1,0:T(8,128)(2,1)S(1)}, bf16[96,128]{1,0:T(8,128)(2,1)S(1)}, u32[]{:S(2)}, u32[]{:S(2)}) collective-permute-start(bf16[96,128]{1,0:T(8,128)(2,1)S(1)} %shard_map.70.refs_8_), channel_id=1, source_target_pairs={{0,16},{8,24},{16,0},{24,8},{1,17},{9,25},{17,1},{25,9},{2,18},{10... | collective-permute-start | bytes 73736 | tf_op jit(solution)/shard_map/ppermute | solution.py:302
  47.0 4.0 %collective-permute-start.14 = (bf16[96,128]{1,0:T(8,128)(2,1)S(1)}, bf16[96,128]{1,0:T(8,128)(2,1)S(1)}, u32[]{:S(2)}, u32[]{:S(2)}) collective-permute-start(bf16[96,128]{1,0:T(8,128)(2,1)S(1)} %shard_map.70.refs_8_), channel_id=1, source_target_pairs={{0,8},{8,0},{16,24},{24,16},{1,9},{9,1},{17,25},{25,17},{2,10},{10... | collective-permute-start | bytes 73736 | tf_op jit(solution)/shard_map/ppermute | solution.py:302
  49.0 5.5 %collective-permute-start.19 = (bf16[96,128]{1,0:T(8,128)(2,1)S(1)}, bf16[96,128]{1,0:T(8,128)(2,1)S(1)}, u32[]{:S(2)}, u32[]{:S(2)}) collective-permute-start(bf16[96,128]{1,0:T(8,128)(2,1)S(1)} %shard_map.76.refs_0_), channel_id=1, source_target_pairs={{0,24},{8,16},{16,8},{24,0},{1,25},{9,17},{17,9},{25,1},{2,26},{10... | collective-permute-start | bytes 73736 | tf_op jit(solution)/shard_map/ppermute | solution.py:302
  50.3 4.2 %collective-permute-start.18 = (bf16[96,128]{1,0:T(8,128)(2,1)S(1)}, bf16[96,128]{1,0:T(8,128)(2,1)S(1)}, u32[]{:S(2)}, u32[]{:S(2)}) collective-permute-start(bf16[96,128]{1,0:T(8,128)(2,1)S(1)} %shard_map.76.refs_0_), channel_id=1, source_target_pairs={{0,16},{8,24},{16,0},{24,8},{1,17},{9,25},{17,1},{25,9},{2,18},{10... | collective-permute-start | bytes 73736 | tf_op jit(solution)/shard_map/ppermute | solution.py:302
  51.0 3.5 %collective-permute-start.17 = (bf16[96,128]{1,0:T(8,128)(2,1)S(1)}, bf16[96,128]{1,0:T(8,128)(2,1)S(1)}, u32[]{:S(2)}, u32[]{:S(2)}) collective-permute-start(bf16[96,128]{1,0:T(8,128)(2,1)S(1)} %shard_map.76.refs_0_), channel_id=1, source_target_pairs={{0,8},{8,0},{16,24},{24,16},{1,9},{9,1},{17,25},{25,17},{2,10},{10... | collective-permute-start | bytes 73736 | tf_op jit(solution)/shard_map/ppermute | solution.py:302

commit v4 on v2

--- a/solution.py
+++ b/solution.py
@@ -187,17 +187,26 @@
     parts = refs[:n_parts]
     turned, *inv, out, held, sems = refs[n_parts:]
     vals = split_rows(total_of(parts))
+    width, feat_dev = held.shape
+
+    def dense(j):
+        return jnp.concatenate([expand(vals, half, j, block) for half in inv], axis=0).astype(BF16)
+
     copies = []
-    for n, j in enumerate(range(0, inv[0].shape[1], block)):
-        pre_grad = jnp.concatenate([expand(vals, half, j, block) for half in inv], axis=0).astype(BF16)
-        for m in range(0, turned.shape[0], tall):
+    pre_grad = dense(0)
+    for j in range(0, feat_dev, block):
+        last = j + block == feat_dev
+        after = None if last else dense(j + block)
+        reach = width // 2 if last else width
+        for m in range(0, width, tall):
             held[m : m + tall, j : j + block] = jnp.dot(
                 turned[m : m + tall, :], pre_grad, preferred_element_type=F32
             ).astype(BF16)
-        copies.append(
-            pltpu.make_async_copy(held.at[:, pl.ds(j, block)], out.at[0, :, pl.ds(j, block)], sems.at[n])
-        )
-        copies[-1].start()
+            if (m + tall) % reach == 0:
+                part = (pl.ds(m + tall - reach, reach), pl.ds(j, block))
+                copies.append(pltpu.make_async_copy(held.at[part], out.at[(0, *part)], sems.at[len(copies)]))
+                copies[-1].start()
+        pre_grad = after
     for copy in copies:
         copy.wait()
 
@@ -332,7 +341,7 @@
     grad_parts = exchange(vals[0])
 
     def out_scratch(rows, columns, block):
-        return [pltpu.VMEM((rows, columns), BF16), pltpu.SemaphoreType.DMA((feat_dev // block,))]
+        return [pltpu.VMEM((rows, columns), BF16), pltpu.SemaphoreType.DMA((feat_dev // block + 1,))]
 
     args = (*e, *pre_parts, *inv, squares)
     dec_grad = call(

time: 58.1 us -> 57.9 us (level)
  no operation moved by 1% of the time
where the time goes in v4:
time: 57.9 us; the launch traced here: 57.8 us
  starting transfers between devices  29.9 us (52%)
  Pallas kernels  19.2 us (33%)
  waiting for transfers between devices  6.97 us (12%)
  local copies, waits for them, and re-layouts  0.91 us (2%)
  between operations  0.83 us (1%)
    ppermute x14, starting transfers between devices, send(): return lax.ppermute(x, 'feat', pairs)  26 us
    pallas_call x10, Pallas kernels, call(): pl.pallas_call(kernel, in_specs=in_specs, out_specs=out_specs, out_shape=...  19.2 us
    ppermute x14, waiting for transfers between devices, send(): return lax.ppermute(x, 'feat', pairs)  6.95 us
    ppermute x6, starting transfers between devices, exchange(): parts.append(lax.ppermute(value, 'layer', pairs))  3.92 us
  transfers between devices with their start and end apart: 20, of which 4 were waited for; matrix products, arithmetic and copies ran while one was open for 0% of the time, Pallas kernels for 27%

profile of v4, /device:TPU:0, one launch (start us, length us, event | category | flops | bytes accessed | tf_op | source)
XLA Modules:
  0.0 57.8 jit_solution(8540033019310360356)
XLA Ops:
  0.6 3.1 %collective-permute-start.7 = (bf16[1,48,2048]{2,1,0:T(8,128)(2,1)}, bf16[1,48,2048]{2,1,0:T(8,128)(2,1)S(1)}, u32[]{:S(2)}, u32[]{:S(2)}) collective-permute-start(bf16[1,48,2048]{2,1,0:T(8,128)(2,1)} %refs_0_.5), channel_id=1, source_target_pairs={{0,2},{1,3},{2,4},{3,5},{4,6},{5,7},{6,0},{7,1},{8,10},{9,11},{10,... | collective-permute-start | bytes 589832 | tf_op jit(solution)/shard_map/ppermute | solution.py:250
  3.7 1.5 %collective-permute-start.12 = (bf16[1,48,2048]{2,1,0:T(8,128)(2,1)}, bf16[1,48,2048]{2,1,0:T(8,128)(2,1)S(1)}, u32[]{:S(2)}, u32[]{:S(2)}) collective-permute-start(bf16[1,48,2048]{2,1,0:T(8,128)(2,1)} %refs_0_.5), channel_id=1, source_target_pairs={{0,1},{1,0},{2,3},{3,2},{4,5},{5,4},{6,7},{7,6},{8,9},{9,8},{10,11... | collective-permute-start | bytes 589832 | tf_op jit(solution)/shard_map/ppermute | solution.py:250
  5.2 2.2 %collective-permute-start.10 = (bf16[1,48,2048]{2,1,0:T(8,128)(2,1)}, bf16[1,48,2048]{2,1,0:T(8,128)(2,1)S(1)}, u32[]{:S(2)}, u32[]{:S(2)}) collective-permute-start(bf16[1,48,2048]{2,1,0:T(8,128)(2,1)} %refs_0_.5), channel_id=1, source_target_pairs={{0,6},{1,7},{2,0},{3,1},{4,2},{5,3},{6,4},{7,5},{8,14},{9,15},{10,... | collective-permute-start | bytes 589832 | tf_op jit(solution)/shard_map/ppermute | solution.py:250
  7.5 1.8 %collective-permute-start.5 = (bf16[1,48,2048]{2,1,0:T(8,128)(2,1)}, bf16[1,48,2048]{2,1,0:T(8,128)(2,1)S(1)}, u32[]{:S(2)}, u32[]{:S(2)}) collective-permute-start(bf16[1,48,2048]{2,1,0:T(8,128)(2,1)} %refs_0_.7), channel_id=1, source_target_pairs={{0,6},{1,7},{2,0},{3,1},{4,2},{5,3},{6,4},{7,5},{8,14},{9,15},{10,... | collective-permute-start | bytes 589832 | tf_op jit(solution)/shard_map/ppermute | solution.py:250
  9.3 0.2 collective-permute-start.1
  9.6 0.8 %copy-done.4 = s32[384,32]{0,1:T(8,128)S(1)} copy-done((s32[384,32]{0,1:T(8,128)S(1)}, s32[384,32]{0,1:T(8,128)}, u32[]{:S(2)}) %copy-start.4) | copy-done | bytes 49176
  10.4 0.8 %shard_map.68.refs_5_.tgt = s32[96,128]{1,0:T(8,128)S(1)} custom-call(s32[9]{0:T(128)S(1)} %stack.39.starts, s32[32,384]{1,0:T(8,128)S(1)} %bitcast.10), custom_call_target="tpu_custom_call" | custom-call | flops 12288 | bytes 196608 | tf_op jit(solution)/shard_map/pallas_call | solution.py:220
  11.2 0.5 collective-permute-done.7.refs_2_
  11.7 6.8 %collective-permute-start.8 = (bf16[1,48,2048]{2,1,0:T(8,128)(2,1)S(1)}, bf16[1,48,2048]{2,1,0:T(8,128)(2,1)S(1)}, u32[]{:S(2)}, u32[]{:S(2)}) collective-permute-start(bf16[1,48,2048]{2,1,0:T(8,128)(2,1)S(1)} %collective-permute-done.7.refs_2_), channel_id=1, source_target_pairs={{0,2},{1,3},{2,4},{3,5},{4,6},{5,7},{6,0},{7,1},{8,10},{9,11},{10,... | collective-permute-start | bytes 589832 | tf_op jit(solution)/shard_map/ppermute | solution.py:250
  18.6 2.5 %shard_map.72.refs_13_.refs_6_ = s32[192,1024]{1,0:T(8,128)S(1)} custom-call(s32[96,128]{1,0:T(8,128)S(1)} %shard_map.68.refs_5_.tgt), custom_call_target="tpu_custom_call" | custom-call | flops 6442450944 | bytes 786432 | tf_op jit(solution)/shard_map/pallas_call | solution.py:220
  21.1 1.9 %collective-permute-start = (bf16[1,48,2048]{2,1,0:T(8,128)(2,1)S(1)}, bf16[1,48,2048]{2,1,0:T(8,128)(2,1)S(1)}, u32[]{:S(2)}, u32[]{:S(2)}) collective-permute-start(bf16[1,48,2048]{2,1,0:T(8,128)(2,1)S(1)} %copy-done.3), channel_id=1, source_target_pairs={{0,1},{1,0},{2,3},{3,2},{4,5},{5,4},{6,7},{7,6},{8,9},{9,8},{10,11... | collective-permute-start | bytes 589832 | tf_op jit(solution)/shard_map/ppermute | solution.py:250
  23.0 0.2 collective-permute-start.13
  23.2 1.8 %collective-permute-start.11 = (bf16[1,48,2048]{2,1,0:T(8,128)(2,1)S(1)}, bf16[1,48,2048]{2,1,0:T(8,128)(2,1)S(1)}, u32[]{:S(2)}, u32[]{:S(2)}) collective-permute-start(bf16[1,48,2048]{2,1,0:T(8,128)(2,1)S(1)} %collective-permute-done.10.refs_2_.refs_6_), channel_id=1, source_target_pairs={{0,1},{1,0},{2,3},{3,2},{4,5},{5,4},{6,7},{7,6},{8,9},{9,8},{10,11... | collective-permute-start | bytes 589832 | tf_op jit(solution)/shard_map/ppermute | solution.py:250
  25.0 1.1 %collective-permute-start.2 = (bf16[1,48,2048]{2,1,0:T(8,128)(2,1)S(1)}, bf16[1,48,2048]{2,1,0:T(8,128)(2,1)S(1)}, u32[]{:S(2)}, u32[]{:S(2)}) collective-permute-start(bf16[1,48,2048]{2,1,0:T(8,128)(2,1)S(1)} %collective-permute-done.1.refs_2_), channel_id=1, source_target_pairs={{0,1},{1,0},{2,3},{3,2},{4,5},{5,4},{6,7},{7,6},{8,9},{9,8},{10,11... | collective-permute-start | bytes 589832 | tf_op jit(solution)/shard_map/ppermute | solution.py:250
  26.1 1.6 %collective-permute-done.8.refs_0_.refs_4_ = bf16[1,48,2048]{2,1,0:T(8,128)(2,1)S(1)} collective-permute-done((bf16[1,48,2048]{2,1,0:T(8,128)(2,1)S(1)}, bf16[1,48,2048]{2,1,0:T(8,128)(2,1)S(1)}, u32[]{:S(2)}, u32[]{:S(2)}) %collective-permute-start.8) | collective-permute-done | bytes 196640 | tf_op jit(solution)/shard_map/ppermute | solution.py:250
  27.7 1.5 %collective-permute-start.9 = (bf16[1,48,2048]{2,1,0:T(8,128)(2,1)S(1)}, bf16[1,48,2048]{2,1,0:T(8,128)(2,1)S(1)}, u32[]{:S(2)}, u32[]{:S(2)}) collective-permute-start(bf16[1,48,2048]{2,1,0:T(8,128)(2,1)S(1)} %collective-permute-done.8.refs_0_.refs_4_), channel_id=1, source_target_pairs={{0,1},{1,0},{2,3},{3,2},{4,5},{5,4},{6,7},{7,6},{8,9},{9,8},{10,11... | collective-permute-start | bytes 589832 | tf_op jit(solution)/shard_map/ppermute | solution.py:250
  29.3 2.5 %shard_map.71.refs_12_.refs_5_ = s32[192,1024]{1,0:T(8,128)S(1)} custom-call(s32[96,128]{1,0:T(8,128)S(1)} %shard_map.68.refs_5_.tgt), custom_call_target="tpu_custom_call" | custom-call | flops 6442450944 | bytes 786432 | tf_op jit(solution)/shard_map/pallas_call | solution.py:220
  31.8 0.7 %collective-permute-start.3 = (bf16[1,48,2048]{2,1,0:T(8,128)(2,1)S(1)}, bf16[1,48,2048]{2,1,0:T(8,128)(2,1)S(1)}, u32[]{:S(2)}, u32[]{:S(2)}) collective-permute-start(bf16[1,48,2048]{2,1,0:T(8,128)(2,1)S(1)} %collective-permute-done.1.refs_2_), channel_id=1, source_target_pairs={{0,2},{1,3},{2,4},{3,5},{4,6},{5,7},{6,0},{7,1},{8,10},{9,11},{10,... | collective-permute-start | bytes 589832 | tf_op jit(solution)/shard_map/ppermute | solution.py:250
  32.5 2.3 %collective-permute-start.6 = (bf16[1,48,2048]{2,1,0:T(8,128)(2,1)S(1)}, bf16[1,48,2048]{2,1,0:T(8,128)(2,1)S(1)}, u32[]{:S(2)}, u32[]{:S(2)}) collective-permute-start(bf16[1,48,2048]{2,1,0:T(8,128)(2,1)S(1)} %collective-permute-done.5.refs_6_.refs_2_), channel_id=1, source_target_pairs={{0,1},{1,0},{2,3},{3,2},{4,5},{5,4},{6,7},{7,6},{8,9},{9,8},{10,11... | collective-permute-start | bytes 589832 | tf_op jit(solution)/shard_map/ppermute | solution.py:250
  34.9 4.6 %collective-permute-done.2.refs_3_ = bf16[1,48,2048]{2,1,0:T(8,128)(2,1)S(1)} collective-permute-done((bf16[1,48,2048]{2,1,0:T(8,128)(2,1)S(1)}, bf16[1,48,2048]{2,1,0:T(8,128)(2,1)S(1)}, u32[]{:S(2)}, u32[]{:S(2)}) %collective-permute-start.2) | collective-permute-done | bytes 196640 | tf_op jit(solution)/shard_map/ppermute | solution.py:250
  39.5 0.8 %collective-permute-start.4 = (bf16[1,48,2048]{2,1,0:T(8,128)(2,1)S(1)}, bf16[1,48,2048]{2,1,0:T(8,128)(2,1)S(1)}, u32[]{:S(2)}, u32[]{:S(2)}) collective-permute-start(bf16[1,48,2048]{2,1,0:T(8,128)(2,1)S(1)} %collective-permute-done.2.refs_3_), channel_id=1, source_target_pairs={{0,2},{1,3},{2,4},{3,5},{4,6},{5,7},{6,0},{7,1},{8,10},{9,11},{10,... | collective-permute-start | bytes 589832 | tf_op jit(solution)/shard_map/ppermute | solution.py:250
  40.2 1.7 %shard_map.75.refs_6_ = f32[96,128]{1,0:T(8,128)S(1)} custom-call(bf16[1,48,2048]{2,1,0:T(8,128)(2,1)S(1)} %copy-done.3, bf16[1,48,2048]{2,1,0:T(8,128)(2,1)S(1)} %collective-permute-done.refs_1_, bf16[1,48,2048]{2,1,0:T(8,128)(2,1)S(1)} %collective-permute-done.1.refs_2_, bf16[1,48,2048]{2,1,0:T(8,128)(2,1)S(1)} %collective-permute-done.2.refs_3_, ...), custom_call_target="tpu_custom_call" | custom-call | flops 805306368 | bytes 786432 | tf_op jit(solution)/shard_map/pallas_call | solution.py:220
  42.0 1.2 %shard_map.69.refs_6_ = f32[96,128]{1,0:T(8,128)S(1)} custom-call(bf16[1,48,2048]{2,1,0:T(8,128)(2,1)S(1)} %copy-done.2, bf16[1,48,2048]{2,1,0:T(8,128)(2,1)S(1)} %collective-permute-done.12.refs_1_, bf16[1,48,2048]{2,1,0:T(8,128)(2,1)S(1)} %collective-permute-done.7.refs_2_, bf16[1,48,2048]{2,1,0:T(8,128)(2,1)S(1)} %collective-permute-done.13.refs_3_, ...), custom_call_target="tpu_custom_call" | custom-call | flops 805306368 | bytes 786432 | tf_op jit(solution)/shard_map/pallas_call | solution.py:220
  43.2 1.2 %shard_map.70.refs_8_ = bf16[96,128]{1,0:T(8,128)(2,1)S(1)} custom-call(bf16[1,48,2048]{2,1,0:T(8,128)(2,1)S(1)} %collective-permute-done.8.refs_0_.refs_4_, bf16[1,48,2048]{2,1,0:T(8,128)(2,1)S(1)} %collective-permute-done.9.refs_1_.refs_5_, bf16[1,48,2048]{2,1,0:T(8,128)(2,1)S(1)} %collective-permute-done.10.refs_2_.refs_6_, ...), custom_call_target="tpu_custom_call" | custom-call | flops 805306368 | bytes 786432 | tf_op jit(solution)/shard_map/pallas_call | solution.py:220
  44.5 1.6 %collective-permute-start.15 = (bf16[96,128]{1,0:T(8,128)(2,1)S(1)}, bf16[96,128]{1,0:T(8,128)(2,1)S(1)}, u32[]{:S(2)}, u32[]{:S(2)}) collective-permute-start(bf16[96,128]{1,0:T(8,128)(2,1)S(1)} %shard_map.70.refs_8_), channel_id=1, source_target_pairs={{0,16},{8,24},{16,0},{24,8},{1,17},{9,25},{17,1},{25,9},{2,18},{10... | collective-permute-start | bytes 73736 | tf_op jit(solution)/shard_map/ppermute | solution.py:307
  46.1 0.5 shard_map.73
  46.6 0.3 collective-permute-start.14
  47.0 1.7 %shard_map.76.refs_0_ = bf16[96,128]{1,0:T(8,128)(2,1)S(1)} custom-call(bf16[1,48,2048]{2,1,0:T(8,128)(2,1)S(1)} %collective-permute-done.3.refs_4_.refs_0_, bf16[1,48,2048]{2,1,0:T(8,128)(2,1)S(1)} %collective-permute-done.4.refs_5_.refs_1_, bf16[1,48,2048]{2,1,0:T(8,128)(2,1)S(1)} %collective-permute-done.5.refs_6_.refs_2_, ...), custom_call_target="tpu_custom_call" | custom-call | flops 805306368 | bytes 786432 | tf_op jit(solution)/shard_map/pallas_call | solution.py:220
  48.7 1.2 %collective-permute-start.19 = (bf16[96,128]{1,0:T(8,128)(2,1)S(1)}, bf16[96,128]{1,0:T(8,128)(2,1)S(1)}, u32[]{:S(2)}, u32[]{:S(2)}) collective-permute-start(bf16[96,128]{1,0:T(8,128)(2,1)S(1)} %shard_map.76.refs_0_), channel_id=1, source_target_pairs={{0,24},{8,16},{16,8},{24,0},{1,25},{9,17},{17,9},{25,1},{2,26},{10... | collective-permute-start | bytes 73736 | tf_op jit(solution)/shard_map/ppermute | solution.py:307
  49.9 0.7 %collective-permute-start.18 = (bf16[96,128]{1,0:T(8,128)(2,1)S(1)}, bf16[96,128]{1,0:T(8,128)(2,1)S(1)}, u32[]{:S(2)}, u32[]{:S(2)}) collective-permute-start(bf16[96,128]{1,0:T(8,128)(2,1)S(1)} %shard_map.76.refs_0_), channel_id=1, source_target_pairs={{0,16},{8,24},{16,0},{24,8},{1,17},{9,25},{17,1},{25,9},{2,18},{10... | collective-permute-start | bytes 73736 | tf_op jit(solution)/shard_map/ppermute | solution.py:307
  50.6 3.6 %shard_map.74 = bf16[1,1024,2048]{2,1,0:T(8,128)(2,1)} custom-call(bf16[1,48,2048]{2,1,0:T(8,128)(2,1)S(1)} %copy-done.3, bf16[1,48,2048]{2,1,0:T(8,128)(2,1)S(1)} %collective-permute-done.refs_1_, bf16[1,48,2048]{2,1,0:T(8,128)(2,1)S(1)} %collective-permute-done.1.refs_2_, bf16[1,48,2048]{2,1,0:T(8,128)(2,1)S(1)} %collective-permute-done.2.refs_3_, ...), custom_call_target="tpu_custom_call" | custom-call | flops 1610612736 | bytes 4194304 | tf_op jit(solution)/shard_map/pallas_call | solution.py:220
  54.3 3.4 %shard_map.77 = bf16[1,2048,1024]{2,1,0:T(8,128)(2,1)} custom-call(bf16[96,128]{1,0:T(8,128)(2,1)S(1)} %shard_map.76.refs_0_, bf16[96,128]{1,0:T(8,128)(2,1)S(1)} %collective-permute-done.17.refs_1_, bf16[96,128]{1,0:T(8,128)(2,1)S(1)} %collective-permute-done.18.refs_2_, bf16[96,128]{1,0:T(8,128)(2,1)S(1)} %collective-permute-done.19.refs_3_, ...), custom_call_target="tpu_custom_call" | custom-call | flops 1610612736 | bytes 4194304 | tf_op jit(solution)/shard_map/pallas_call | solution.py:220
  (29 shorter events, 0.4 us)
Async XLA Ops:
  0.6 11.1 %collective-permute-start.7 = (bf16[1,48,2048]{2,1,0:T(8,128)(2,1)}, bf16[1,48,2048]{2,1,0:T(8,128)(2,1)S(1)}, u32[]{:S(2)}, u32[]{:S(2)}) collective-permute-start(bf16[1,48,2048]{2,1,0:T(8,128)(2,1)} %refs_0_.5), channel_id=1, source_target_pairs={{0,2},{1,3},{2,4},{3,5},{4,6},{5,7},{6,0},{7,1},{8,10},{9,11},{10,... | collective-permute-start | bytes 589832 | tf_op jit(solution)/shard_map/ppermute | solution.py:250
  3.7 17.4 %collective-permute-start.12 = (bf16[1,48,2048]{2,1,0:T(8,128)(2,1)}, bf16[1,48,2048]{2,1,0:T(8,128)(2,1)S(1)}, u32[]{:S(2)}, u32[]{:S(2)}) collective-permute-start(bf16[1,48,2048]{2,1,0:T(8,128)(2,1)} %refs_0_.5), channel_id=1, source_target_pairs={{0,1},{1,0},{2,3},{3,2},{4,5},{5,4},{6,7},{7,6},{8,9},{9,8},{10,11... | collective-permute-start | bytes 589832 | tf_op jit(solution)/shard_map/ppermute | solution.py:250
  5.2 17.8 %collective-permute-start.10 = (bf16[1,48,2048]{2,1,0:T(8,128)(2,1)}, bf16[1,48,2048]{2,1,0:T(8,128)(2,1)S(1)}, u32[]{:S(2)}, u32[]{:S(2)}) collective-permute-start(bf16[1,48,2048]{2,1,0:T(8,128)(2,1)} %refs_0_.5), channel_id=1, source_target_pairs={{0,6},{1,7},{2,0},{3,1},{4,2},{5,3},{6,4},{7,5},{8,14},{9,15},{10,... | collective-permute-start | bytes 589832 | tf_op jit(solution)/shard_map/ppermute | solution.py:250
  7.5 15.7 %collective-permute-start.5 = (bf16[1,48,2048]{2,1,0:T(8,128)(2,1)}, bf16[1,48,2048]{2,1,0:T(8,128)(2,1)S(1)}, u32[]{:S(2)}, u32[]{:S(2)}) collective-permute-start(bf16[1,48,2048]{2,1,0:T(8,128)(2,1)} %refs_0_.7), channel_id=1, source_target_pairs={{0,6},{1,7},{2,0},{3,1},{4,2},{5,3},{6,4},{7,5},{8,14},{9,15},{10,... | collective-permute-start | bytes 589832 | tf_op jit(solution)/shard_map/ppermute | solution.py:250
  9.3 15.8 %collective-permute-start.1 = (bf16[1,48,2048]{2,1,0:T(8,128)(2,1)}, bf16[1,48,2048]{2,1,0:T(8,128)(2,1)S(1)}, u32[]{:S(2)}, u32[]{:S(2)}) collective-permute-start(bf16[1,48,2048]{2,1,0:T(8,128)(2,1)} %refs_0_.7), channel_id=1, source_target_pairs={{0,2},{1,3},{2,4},{3,5},{4,6},{5,7},{6,0},{7,1},{8,10},{9,11},{10,... | collective-permute-start | bytes 589832 | tf_op jit(solution)/shard_map/ppermute | solution.py:250
  9.6 0.8 %copy-start.4 = (s32[384,32]{0,1:T(8,128)S(1)}, s32[384,32]{0,1:T(8,128)}, u32[]{:S(2)}) copy-start(s32[384,32]{0,1:T(8,128)} %param.9) | copy-start | bytes 147460
  11.2 9.9 %copy-start.3 = (bf16[1,48,2048]{2,1,0:T(8,128)(2,1)S(1)}, bf16[1,48,2048]{2,1,0:T(8,128)(2,1)}, u32[]{:S(2)}) copy-start(bf16[1,48,2048]{2,1,0:T(8,128)(2,1)} %refs_0_.7) | copy-start | bytes 589828
  11.7 16.0 %collective-permute-start.8 = (bf16[1,48,2048]{2,1,0:T(8,128)(2,1)S(1)}, bf16[1,48,2048]{2,1,0:T(8,128)(2,1)S(1)}, u32[]{:S(2)}, u32[]{:S(2)}) collective-permute-start(bf16[1,48,2048]{2,1,0:T(8,128)(2,1)S(1)} %collective-permute-done.7.refs_2_), channel_id=1, source_target_pairs={{0,2},{1,3},{2,4},{3,5},{4,6},{5,7},{6,0},{7,1},{8,10},{9,11},{10,... | collective-permute-start | bytes 589832 | tf_op jit(solution)/shard_map/ppermute | solution.py:250
  21.1 19.2 %copy-start.1 = (bf16[1,1024,2048]{2,1,0:T(8,128)(2,1)S(1)}, bf16[1,1024,2048]{2,1,0:T(8,128)(2,1)}, u32[]{:S(2)}) copy-start(bf16[1,1024,2048]{2,1,0:T(8,128)(2,1)} %refs_4_.7) | copy-start | bytes 12582916
  21.1 10.7 %collective-permute-start = (bf16[1,48,2048]{2,1,0:T(8,128)(2,1)S(1)}, bf16[1,48,2048]{2,1,0:T(8,128)(2,1)S(1)}, u32[]{:S(2)}, u32[]{:S(2)}) collective-permute-start(bf16[1,48,2048]{2,1,0:T(8,128)(2,1)S(1)} %copy-done.3), channel_id=1, source_target_pairs={{0,1},{1,0},{2,3},{3,2},{4,5},{5,4},{6,7},{7,6},{8,9},{9,8},{10,11... | collective-permute-start | bytes 589832 | tf_op jit(solution)/shard_map/ppermute | solution.py:250
  23.0 9.5 %collective-permute-start.13 = (bf16[1,48,2048]{2,1,0:T(8,128)(2,1)S(1)}, bf16[1,48,2048]{2,1,0:T(8,128)(2,1)S(1)}, u32[]{:S(2)}, u32[]{:S(2)}) collective-permute-start(bf16[1,48,2048]{2,1,0:T(8,128)(2,1)S(1)} %collective-permute-done.7.refs_2_), channel_id=1, source_target_pairs={{0,1},{1,0},{2,3},{3,2},{4,5},{5,4},{6,7},{7,6},{8,9},{9,8},{10,11... | collective-permute-start | bytes 589832 | tf_op jit(solution)/shard_map/ppermute | solution.py:250
  23.2 20.0 %collective-permute-start.11 = (bf16[1,48,2048]{2,1,0:T(8,128)(2,1)S(1)}, bf16[1,48,2048]{2,1,0:T(8,128)(2,1)S(1)}, u32[]{:S(2)}, u32[]{:S(2)}) collective-permute-start(bf16[1,48,2048]{2,1,0:T(8,128)(2,1)S(1)} %collective-permute-done.10.refs_2_.refs_6_), channel_id=1, source_target_pairs={{0,1},{1,0},{2,3},{3,2},{4,5},{5,4},{6,7},{7,6},{8,9},{9,8},{10,11... | collective-permute-start | bytes 589832 | tf_op jit(solution)/shard_map/ppermute | solution.py:250
  25.0 14.4 %collective-permute-start.2 = (bf16[1,48,2048]{2,1,0:T(8,128)(2,1)S(1)}, bf16[1,48,2048]{2,1,0:T(8,128)(2,1)S(1)}, u32[]{:S(2)}, u32[]{:S(2)}) collective-permute-start(bf16[1,48,2048]{2,1,0:T(8,128)(2,1)S(1)} %collective-permute-done.1.refs_2_), channel_id=1, source_target_pairs={{0,1},{1,0},{2,3},{3,2},{4,5},{5,4},{6,7},{7,6},{8,9},{9,8},{10,11... | collective-permute-start | bytes 589832 | tf_op jit(solution)/shard_map/ppermute | solution.py:250
  27.7 15.5 %collective-permute-start.9 = (bf16[1,48,2048]{2,1,0:T(8,128)(2,1)S(1)}, bf16[1,48,2048]{2,1,0:T(8,128)(2,1)S(1)}, u32[]{:S(2)}, u32[]{:S(2)}) collective-permute-start(bf16[1,48,2048]{2,1,0:T(8,128)(2,1)S(1)} %collective-permute-done.8.refs_0_.refs_4_), channel_id=1, source_target_pairs={{0,1},{1,0},{2,3},{3,2},{4,5},{5,4},{6,7},{7,6},{8,9},{9,8},{10,11... | collective-permute-start | bytes 589832 | tf_op jit(solution)/shard_map/ppermute | solution.py:250
  31.8 10.2 %copy-start = (bf16[1,2048,1024]{2,1,0:T(8,128)(2,1)S(1)}, bf16[1,2048,1024]{2,1,0:T(8,128)(2,1)}, u32[]{:S(2)}) copy-start(bf16[1,2048,1024]{2,1,0:T(8,128)(2,1)} %refs_4_.5) | copy-start | bytes 12582916
  31.8 10.2 %copy-start.2 = (bf16[1,48,2048]{2,1,0:T(8,128)(2,1)S(1)}, bf16[1,48,2048]{2,1,0:T(8,128)(2,1)}, u32[]{:S(2)}) copy-start(bf16[1,48,2048]{2,1,0:T(8,128)(2,1)} %refs_0_.5) | copy-start | bytes 589828
  31.8 15.1 %collective-permute-start.3 = (bf16[1,48,2048]{2,1,0:T(8,128)(2,1)S(1)}, bf16[1,48,2048]{2,1,0:T(8,128)(2,1)S(1)}, u32[]{:S(2)}, u32[]{:S(2)}) collective-permute-start(bf16[1,48,2048]{2,1,0:T(8,128)(2,1)S(1)} %collective-permute-done.1.refs_2_), channel_id=1, source_target_pairs={{0,2},{1,3},{2,4},{3,5},{4,6},{5,7},{6,0},{7,1},{8,10},{9,11},{10,... | collective-permute-start | bytes 589832 | tf_op jit(solution)/shard_map/ppermute | solution.py:250
  32.5 14.0 %collective-permute-start.6 = (bf16[1,48,2048]{2,1,0:T(8,128)(2,1)S(1)}, bf16[1,48,2048]{2,1,0:T(8,128)(2,1)S(1)}, u32[]{:S(2)}, u32[]{:S(2)}) collective-permute-start(bf16[1,48,2048]{2,1,0:T(8,128)(2,1)S(1)} %collective-permute-done.5.refs_6_.refs_2_), channel_id=1, source_target_pairs={{0,1},{1,0},{2,3},{3,2},{4,5},{5,4},{6,7},{7,6},{8,9},{9,8},{10,11... | collective-permute-start | bytes 589832 | tf_op jit(solution)/shard_map/ppermute | solution.py:250
  39.5 7.5 %collective-permute-start.4 = (bf16[1,48,2048]{2,1,0:T(8,128)(2,1)S(1)}, bf16[1,48,2048]{2,1,0:T(8,128)(2,1)S(1)}, u32[]{:S(2)}, u32[]{:S(2)}) collective-permute-start(bf16[1,48,2048]{2,1,0:T(8,128)(2,1)S(1)} %collective-permute-done.2.refs_3_), channel_id=1, source_target_pairs={{0,2},{1,3},{2,4},{3,5},{4,6},{5,7},{6,0},{7,1},{8,10},{9,11},{10,... | collective-permute-start | bytes 589832 | tf_op jit(solution)/shard_map/ppermute | solution.py:250
  44.4 6.2 %collective-permute-start.16 = (bf16[96,128]{1,0:T(8,128)(2,1)S(1)}, bf16[96,128]{1,0:T(8,128)(2,1)S(1)}, u32[]{:S(2)}, u32[]{:S(2)}) collective-permute-start(bf16[96,128]{1,0:T(8,128)(2,1)S(1)} %shard_map.70.refs_8_), channel_id=1, source_target_pairs={{0,24},{8,16},{16,8},{24,0},{1,25},{9,17},{17,9},{25,1},{2,26},{10... | collective-permute-start | bytes 73736 | tf_op jit(solution)/shard_map/ppermute | solution.py:307
  44.5 6.2 %collective-permute-start.15 = (bf16[96,128]{1,0:T(8,128)(2,1)S(1)}, bf16[96,128]{1,0:T(8,128)(2,1)S(1)}, u32[]{:S(2)}, u32[]{:S(2)}) collective-permute-start(bf16[96,128]{1,0:T(8,128)(2,1)S(1)} %shard_map.70.refs_8_), channel_id=1, source_target_pairs={{0,16},{8,24},{16,0},{24,8},{1,17},{9,25},{17,1},{25,9},{2,18},{10... | collective-permute-start | bytes 73736 | tf_op jit(solution)/shard_map/ppermute | solution.py:307
  46.6 4.1 %collective-permute-start.14 = (bf16[96,128]{1,0:T(8,128)(2,1)S(1)}, bf16[96,128]{1,0:T(8,128)(2,1)S(1)}, u32[]{:S(2)}, u32[]{:S(2)}) collective-permute-start(bf16[96,128]{1,0:T(8,128)(2,1)S(1)} %shard_map.70.refs_8_), channel_id=1, source_target_pairs={{0,8},{8,0},{16,24},{24,16},{1,9},{9,1},{17,25},{25,17},{2,10},{10... | collective-permute-start | bytes 73736 | tf_op jit(solution)/shard_map/ppermute | solution.py:307
  48.7 5.6 %collective-permute-start.19 = (bf16[96,128]{1,0:T(8,128)(2,1)S(1)}, bf16[96,128]{1,0:T(8,128)(2,1)S(1)}, u32[]{:S(2)}, u32[]{:S(2)}) collective-permute-start(bf16[96,128]{1,0:T(8,128)(2,1)S(1)} %shard_map.76.refs_0_), channel_id=1, source_target_pairs={{0,24},{8,16},{16,8},{24,0},{1,25},{9,17},{17,9},{25,1},{2,26},{10... | collective-permute-start | bytes 73736 | tf_op jit(solution)/shard_map/ppermute | solution.py:307
  49.9 4.4 %collective-permute-start.18 = (bf16[96,128]{1,0:T(8,128)(2,1)S(1)}, bf16[96,128]{1,0:T(8,128)(2,1)S(1)}, u32[]{:S(2)}, u32[]{:S(2)}) collective-permute-start(bf16[96,128]{1,0:T(8,128)(2,1)S(1)} %shard_map.76.refs_0_), channel_id=1, source_target_pairs={{0,16},{8,24},{16,0},{24,8},{1,17},{9,25},{17,1},{25,9},{2,18},{10... | collective-permute-start | bytes 73736 | tf_op jit(solution)/shard_map/ppermute | solution.py:307
  50.6 3.7 %collective-permute-start.17 = (bf16[96,128]{1,0:T(8,128)(2,1)S(1)}, bf16[96,128]{1,0:T(8,128)(2,1)S(1)}, u32[]{:S(2)}, u32[]{:S(2)}) collective-permute-start(bf16[96,128]{1,0:T(8,128)(2,1)S(1)} %shard_map.76.refs_0_), channel_id=1, source_target_pairs={{0,8},{8,0},{16,24},{24,16},{1,9},{9,1},{17,25},{25,17},{2,10},{10... | collective-permute-start | bytes 73736 | tf_op jit(solution)/shard_map/ppermute | solution.py:307
